TPU v7x, 128 devices: a whole 4x4x4 slice. The times are simulated.
128 devices in a mesh: row: 4 (over x), col: 32 (over y, z, core).
Axes of the slice: x: 4, y: 4, z: 4, core: 2. Of those that a mesh axis runs over, the one named last changes fastest.
Arguments:
- object_slices: float32 [4, 2, 2048, 8192], P(None, None, 'row', 'col'), may hold values from -4 to 4
- probe_wave: float32 [2, 256, 256], replicated, may hold values from -5 to 5
- propagator_phase: float32 [256, 256], replicated, may hold values from -3.140625 to 3.140625
- positions: int32 [384, 2], P(('row', 'col')), may hold values from 0 to 511, as said below
- slot_count: int32 [128], P(('row', 'col')), may hold values from 1 to 3, as said below
- intensity: float32 [384, 256, 256], P(('row', 'col')), may hold values from 0 to 2
Outputs:
- object_grad: float32 [4, 2, 2048, 8192], P(None, None, 'row', 'col')
- probe_grad: float32 [2, 256, 256], replicated
Inputs may be any that keep to these rules, and one draw needn't show every extreme that they name: positions[g, 0] is below 512 and positions[g, 1] below 256; slots are ordered by owner device, owners in row-major order of the mesh. Slot k of owner d is in use when k < slot_count[d].
All inputs are finite; a program needn't handle non-finite values.
Results may differ from a plain program's by a relative error of at most 0.0002.
Values sent between devices are 32-bit elements; how exact they have to be, the bound alone decides.
No kernel may reach another device: no remote copies, remote signals or barrier semaphores. Data moves between devices by JAX's collectives and lax.ppermute only.
A program may use at most 128 MiB of HBM per device.

v0:
```python
import functools
import math

import jax
import jax.numpy as jnp
import numpy as np
from jax import lax
from jax.experimental import pallas as pl
from jax.experimental.pallas import tpu as pltpu
from jax.sharding import PartitionSpec as P


WIN = 256
HALF = 128
F32 = jnp.float32
BF16 = jnp.bfloat16


def shift(x, axis, by):
    devices = lax.axis_size(axis)
    pairs = [(i, i + by) for i in range(devices) if 0 <= i + by < devices]
    return lax.ppermute(x, axis, pairs)


def dft_tables():
    n = np.arange(HALF)
    even = 2.0 * math.pi * ((2 * np.outer(n, n)) % WIN) / WIN
    odd = 2.0 * math.pi * ((np.outer(n, 2 * n + 1)) % WIN) / WIN
    tables = []
    for angle in (even, odd):
        cos, sin = np.cos(angle) / 16.0, np.sin(angle) / 16.0
        table = np.block([[cos, -sin], [sin, cos]])
        tables += [table, table.T]
    whole = np.stack(tables).astype(np.float32)
    high = whole.astype(jnp.bfloat16)
    low = (whole - high.astype(np.float32)).astype(jnp.bfloat16)
    return np.stack([high, low], axis=1)


def split(x):
    high = x.astype(BF16)
    low = (x - high.astype(F32)).astype(BF16)
    return high, low


def right_mul(x, tab, index):
    high, low = split(x)
    t_high, t_low = tab[index, 0], tab[index, 1]
    return jnp.dot(
        jnp.concatenate([high, low, high], axis=1),
        jnp.concatenate([t_high, t_high, t_low], axis=0),
        preferred_element_type=F32,
    )


def left_mul(x, tab, index):
    high, low = split(x)
    t_high, t_low = tab[index, 0], tab[index, 1]
    return jnp.dot(
        jnp.concatenate([t_high, t_high, t_low], axis=1),
        jnp.concatenate([high, low, high], axis=0),
        preferred_element_type=F32,
    )


EVEN, EVEN_T, ODD, ODD_T = range(4)


def forward2d(re, im, tab):
    re0, re1, im0, im1 = re[:, :HALF], re[:, HALF:], im[:, :HALF], im[:, HALF:]
    even = right_mul(jnp.concatenate([re0 + re1, im0 + im1], axis=1), tab, EVEN)
    odd = right_mul(jnp.concatenate([re0 - re1, im0 - im1], axis=1), tab, ODD)
    re = jnp.concatenate([even[:, :HALF], odd[:, :HALF]], axis=1)
    im = jnp.concatenate([even[:, HALF:], odd[:, HALF:]], axis=1)
    re0, re1, im0, im1 = re[:HALF], re[HALF:], im[:HALF], im[HALF:]
    even = left_mul(jnp.concatenate([re0 + re1, im0 + im1], axis=0), tab, EVEN_T)
    odd = left_mul(jnp.concatenate([re0 - re1, im0 - im1], axis=0), tab, ODD_T)
    return even, odd


def inverse2d(even, odd, tab):
    a = left_mul(even, tab, EVEN)
    b = left_mul(odd, tab, ODD)
    plus, minus = a + b, a - b
    re = jnp.concatenate([plus[:HALF], minus[:HALF]], axis=0)
    im = jnp.concatenate([plus[HALF:], minus[HALF:]], axis=0)
    a = right_mul(jnp.concatenate([re[:, :HALF], im[:, :HALF]], axis=1), tab, EVEN_T)
    b = right_mul(jnp.concatenate([re[:, HALF:], im[:, HALF:]], axis=1), tab, ODD_T)
    plus, minus = a + b, a - b
    re = jnp.concatenate([plus[:, :HALF], minus[:, :HALF]], axis=1)
    im = jnp.concatenate([plus[:, HALF:], minus[:, HALF:]], axis=1)
    return re, im


def propagate(re, im, tab, kern, sign):
    halves = forward2d(re, im, tab)
    moved = []
    for parity in range(2):
        f_re, f_im = halves[parity][:HALF], halves[parity][HALF:]
        k_re, k_im = kern[parity, 0], kern[parity, 1] * sign
        moved.append(
            jnp.concatenate([k_re * f_re - k_im * f_im, k_re * f_im + k_im * f_re], axis=0)
        )
    return inverse2d(moved[0], moved[1], tab)


def far_adjoint(re, im, tab, measured, used):
    halves = forward2d(re, im, tab)
    moved = []
    for parity in range(2):
        f_re, f_im = halves[parity][:HALF], halves[parity][HALF:]
        weight = (f_re * f_re + f_im * f_im - measured[0, parity]) * used
        moved.append(jnp.concatenate([weight * f_re, weight * f_im], axis=0))
    return inverse2d(moved[0], moved[1], tab)


def cut(ext, part, row, col):
    base = col // HALF
    lane = col % HALF
    keep = lax.broadcasted_iota(jnp.int32, (WIN, HALF), 1) < HALF - lane
    back = (HALF - lane) % HALF
    turned = [pltpu.roll(ext[part, base + j, pl.ds(row, WIN), :], back, 1) for j in range(3)]
    return jnp.concatenate(
        [jnp.where(keep, turned[0], turned[1]), jnp.where(keep, turned[1], turned[2])], axis=1
    )


def add_back(ext, part, row, col, value):
    base = col // HALF
    lane = col % HALF
    keep = lax.broadcasted_iota(jnp.int32, (WIN, HALF), 1) >= lane
    zero = jnp.zeros((WIN, HALF), F32)
    turned = [pltpu.roll(value[:, j * HALF : (j + 1) * HALF], lane, 1) for j in range(2)]
    wide = [
        jnp.where(keep, turned[0], zero),
        jnp.where(keep, turned[1], turned[0]),
        jnp.where(keep, zero, turned[1]),
    ]
    for j in range(3):
        place = (part, base + j, pl.ds(row, WIN), slice(None))
        ext[place] = ext[place] + wide[j]


def gather_ext(own, lower, sides, ext):
    for j in range(2):
        lanes = slice(j * HALF, (j + 1) * HALF)
        ext[:, j, :512] = own[0, :, :, lanes]
        ext[:, j, 512:] = lower[:, :, lanes]
        top = 0
        for side in sides:
            rows = side.shape[1]
            ext[:, 2 + j, top : top + rows] = side[:, :, lanes]
            top += rows


def spread_ext(ext, own, lower, sides):
    for j in range(2):
        lanes = slice(j * HALF, (j + 1) * HALF)
        own[:, :, lanes] = ext[:, j, :512]
        lower[:, :, lanes] = ext[:, j, 512:]
        top = 0
        for side in sides:
            rows = side.shape[1]
            side[:, :, lanes] = ext[:, 2 + j, top : top + rows]
            top += rows


def forward_kernel(side_count, pos, own, lower, *refs):
    sides, (wave, tab, kern, slab_out, wave_out, ext) = refs[:side_count], refs[side_count:]
    slot = pl.program_id(0)

    @pl.when(slot == 0)
    def _():
        gather_ext(own, lower, sides, ext)

    row, col = pos[slot, 0], pos[slot, 1]
    s_re, s_im = cut(ext, 0, row, col), cut(ext, 1, row, col)
    slab_out[0, 0], slab_out[0, 1] = s_re, s_im
    w_re, w_im = wave[0, 0], wave[0, 1]
    wave_out[0, 0], wave_out[0, 1] = propagate(
        w_re * s_re - w_im * s_im, w_re * s_im + w_im * s_re, tab, kern, 1.0
    )


def turn_kernel(side_count, pos, count, own, lower, *refs):
    sides, (wave, tab, measured, g_own, g_lower, g_side, g_wave, ext, g_ext) = (
        refs[:side_count], refs[side_count:]
    )
    slot = pl.program_id(0)

    @pl.when(slot == 0)
    def _():
        gather_ext(own, lower, sides, ext)
        g_ext[...] = jnp.zeros(g_ext.shape, F32)

    row, col = pos[slot, 0], pos[slot, 1]
    used = jnp.where(slot < count[0], 1.0, 0.0).astype(F32)
    s_re, s_im = cut(ext, 0, row, col), cut(ext, 1, row, col)
    w_re, w_im = wave[0, 0], wave[0, 1]
    e_re, e_im = far_adjoint(
        w_re * s_re - w_im * s_im, w_re * s_im + w_im * s_re, tab, measured, used
    )
    add_back(g_ext, 0, row, col, w_re * e_re + w_im * e_im)
    add_back(g_ext, 1, row, col, w_re * e_im - w_im * e_re)
    g_wave[0, 0] = s_re * e_re + s_im * e_im
    g_wave[0, 1] = s_re * e_im - s_im * e_re

    @pl.when(slot == pl.num_programs(0) - 1)
    def _():
        spread_ext(g_ext, g_own, g_lower, [g_side])


def backward_kernel(first, pos, slab, wave, g_next, tab, kern, g_own, g_lower, *refs):
    sides, (g_wave, g_ext) = refs[:-2], refs[-2:]
    slot = pl.program_id(0)

    @pl.when(slot == 0)
    def _():
        g_ext[...] = jnp.zeros(g_ext.shape, F32)
        if first:
            g_wave[...] = jnp.zeros(g_wave.shape, F32)

    row, col = pos[slot, 0], pos[slot, 1]
    s_re, s_im = slab[0, 0], slab[0, 1]
    w_re, w_im = wave[0, 0], wave[0, 1]
    e_re, e_im = propagate(g_next[0, 0], g_next[0, 1], tab, kern, -1.0)
    add_back(g_ext, 0, row, col, w_re * e_re + w_im * e_im)
    add_back(g_ext, 1, row, col, w_re * e_im - w_im * e_re)
    p_re = s_re * e_re + s_im * e_im
    p_im = s_re * e_im - s_im * e_re
    if first:
        g_wave[0, 0] += p_re
        g_wave[0, 1] += p_im
    else:
        g_wave[0, 0], g_wave[0, 1] = p_re, p_im

    @pl.when(slot == pl.num_programs(0) - 1)
    def _():
        spread_ext(g_ext, g_own, g_lower, sides)


def whole(*shape):
    return pl.BlockSpec(shape, lambda slot, *_: (0,) * len(shape))


def by_slot(*shape):
    return pl.BlockSpec((1,) + shape, lambda slot, *_: (slot,) + (0,) * len(shape))


TILE = (2, 512, 256)
STRIP = (2, 256, 256)
SIDE = (2, 768, 256)
PARAMS = pltpu.CompilerParams(dimension_semantics=("arbitrary",), vmem_limit_bytes=56 << 20)
COST = pl.CostEstimate(flops=10 * 1000 * 1000 * 1000, bytes_accessed=12 << 20, transcendentals=0)
EXT = pltpu.VMEM((2, 4, 768, HALF), F32)
TABLES = (4, 2, 256, 256)


def arr(*shape):
    return jax.ShapeDtypeStruct(shape, F32)


def tile_of(layer):
    return pl.BlockSpec((1,) + TILE, lambda slot, *_: (layer, 0, 0, 0))


def run_forward(layer, slots, pos, tiles, lower, sides, wave, tab, kern):
    shared = wave.shape[0] == 1
    return pl.pallas_call(
        functools.partial(forward_kernel, len(sides)),
        grid_spec=pltpu.PrefetchScalarGridSpec(
            num_scalar_prefetch=1,
            grid=(slots,),
            in_specs=[tile_of(layer), whole(*STRIP), *[whole(*side.shape) for side in sides],
                      whole(1, *STRIP) if shared else by_slot(*STRIP),
                      whole(*TABLES), whole(2, 2, HALF, WIN)],
            out_specs=[by_slot(*STRIP), by_slot(*STRIP)],
            scratch_shapes=[EXT],
        ),
        out_shape=[arr(slots, *STRIP), arr(slots, *STRIP)],
        compiler_params=PARAMS,
        cost_estimate=COST,
        name="forward",
    )(pos, tiles, lower, *sides, wave, tab, kern)


def run_turn(layer, slots, pos, count, tiles, lower, sides, wave, tab, measured):
    return pl.pallas_call(
        functools.partial(turn_kernel, len(sides)),
        grid_spec=pltpu.PrefetchScalarGridSpec(
            num_scalar_prefetch=2,
            grid=(slots,),
            in_specs=[tile_of(layer), whole(*STRIP), *[whole(*side.shape) for side in sides],
                      by_slot(*STRIP), whole(*TABLES), by_slot(2, HALF, WIN)],
            out_specs=[whole(*TILE), whole(*STRIP), whole(*SIDE), by_slot(*STRIP)],
            scratch_shapes=[EXT, EXT],
        ),
        out_shape=[arr(*TILE), arr(*STRIP), arr(*SIDE), arr(slots, *STRIP)],
        compiler_params=PARAMS,
        cost_estimate=COST,
        name="turn",
    )(pos, count, tiles, lower, *sides, wave, tab, measured)


def run_backward(slots, pos, slab, wave, g_next, tab, kern, first):
    shared = wave.shape[0] == 1
    sides = [TILE, STRIP] if first else [SIDE]
    return pl.pallas_call(
        functools.partial(backward_kernel, first),
        grid_spec=pltpu.PrefetchScalarGridSpec(
            num_scalar_prefetch=1,
            grid=(slots,),
            in_specs=[by_slot(*STRIP), whole(1, *STRIP) if shared else by_slot(*STRIP),
                      by_slot(*STRIP), whole(*TABLES), whole(2, 2, HALF, WIN)],
            out_specs=[whole(*TILE), whole(*STRIP), *[whole(*side) for side in sides],
                       whole(1, *STRIP) if first else by_slot(*STRIP)],
            scratch_shapes=[EXT],
        ),
        out_shape=[arr(*TILE), arr(*STRIP), *[arr(*side) for side in sides],
                   arr(1 if first else slots, *STRIP)],
        compiler_params=PARAMS,
        cost_estimate=COST,
        name="backward",
    )(pos, slab, wave, g_next, tab, kern)


def parity_order(x):
    order = np.concatenate([np.arange(0, WIN, 2), np.arange(1, WIN, 2)])
    pick = jnp.asarray(np.eye(WIN, dtype=np.float32)[order])
    high = lax.Precision.HIGHEST
    x = jnp.einsum("...rc,dc->...rd", x, pick, precision=high)
    return jnp.einsum("er,...rd->...ed", pick, x, precision=high)


def turn_by(x, axis, by):
    sizes = {"x": lax.axis_size("row"), "y": 4, "z": 4, "core": 2}
    pairs = []
    for x_at in range(sizes["x"]):
        for y_at in range(4):
            for z_at in range(4):
                for core in range(2):
                    place = {"x": x_at, "y": y_at, "z": z_at, "core": core}
                    there = dict(place)
                    there[axis] = (place[axis] + by) % sizes[axis]
                    pairs.append(tuple(
                        p["x"] * 32 + p["y"] * 8 + p["z"] * 2 + p["core"] for p in (place, there)
                    ))
    return lax.ppermute(x, ("row", "col"), pairs)


def sum_over_devices(x):
    shape = x.shape
    part = x.reshape(512, 256)
    col = lax.axis_index("col")
    place = {"core": (col % 2, 2), "y": (col // 8, 4)}
    for axis in ("core", "y"):
        me, size = place[axis]
        rows = part.shape[0] // size
        total = lax.dynamic_slice_in_dim(part, me * rows, rows)
        for by in range(1, size):
            block = lax.dynamic_slice_in_dim(part, (me + by) % size * rows, rows)
            other = turn_by(block, axis, by)
            total = total + other
        part = total
    for axis in ("x", "z"):
        others = [turn_by(part, axis, by) for by in (1, 2, 3)]
        part = part + others[0] + others[1] + others[2]
    for axis in ("y", "core"):
        me, size = place[axis]
        rows = part.shape[0]
        joined = jnp.zeros((rows * size, 256), F32)
        joined = lax.dynamic_update_slice_in_dim(joined, part, me * rows, 0)
        for by in range(1, size):
            other = turn_by(part, axis, by)
            joined = lax.dynamic_update_slice_in_dim(
                joined, other, (me - by) % size * rows, 0
            )
        part = joined
    return part.reshape(shape)


def work(tiles, probe_wave, propagator_phase, positions, slot_count, intensity):
    layers = tiles.shape[0]
    slots = positions.shape[0]
    last = layers - 1
    strip = tiles[0, :, :WIN]
    lowers = [shift(strip, "row", -1)]
    rest, strip = lax.optimization_barrier((tiles, strip))
    right = shift(rest[0], "col", -1)
    for layer in range(1, layers):
        lowers.append(shift(rest[layer, :, :WIN], "row", -1))
    tab = jnp.asarray(dft_tables())
    phase = parity_order(propagator_phase).reshape(2, 1, HALF, WIN)
    kern = jnp.concatenate([jnp.cos(phase), jnp.sin(phase)], axis=1)
    measured = parity_order(intensity).reshape(slots, 2, HALF, WIN)
    corner = shift(lowers[0], "col", -1)
    sides = [(right, corner)]
    for layer in range(1, layers):
        joined = jnp.concatenate([rest[layer], lowers[layer]], axis=1)
        sides.append((shift(joined, "col", -1),))
    waves = [probe_wave[None]]
    slabs = []
    for layer in range(last):
        slab, wave = run_forward(
            layer, slots, positions, tiles, lowers[layer], sides[layer], waves[layer], tab, kern
        )
        slabs.append(slab)
        waves.append(wave)
    grads = [None] * layers
    *grads[last], g_wave = run_turn(
        last, slots, positions, slot_count, tiles, lowers[last], sides[last], waves[last],
        tab, measured
    )
    for layer in reversed(range(last)):
        *grads[layer], g_wave = run_backward(
            slots, positions, slabs[layer], waves[layer], g_wave, tab, kern, layer == 0
        )
    outs = [None] * layers
    for layer in reversed(range(layers)):
        own, lower, *side = grads[layer]
        if layer:
            back = shift(side[0], "col", 1)
            right, corner = back[:, :512], back[:, 512:]
        else:
            corner = shift(side[1], "col", 1)
            right = shift(side[0], "col", 1)
        below = shift(lower + corner, "row", 1)
        outs[layer] = (own + right).at[:, :WIN].add(below)
    probe = sum_over_devices(g_wave[0])
    return (jnp.stack(outs), probe)


def solution(mesh):
    placed = (
        P(None, None, "row", "col"),
        P(),
        P(),
        P(("row", "col"), None),
        P(("row", "col")),
        P(("row", "col"), None, None),
    )
    return jax.shard_map(
        work,
        mesh=mesh,
        in_specs=placed,
        out_specs=(P(None, None, "row", "col"), P()),
        check_vma=False,
    )
```

profile of v0, /device:TPU:100, one launch (start us, length us, event | category | flops | bytes accessed | tf_op | source)
XLA Modules:
  0.0 304.6 jit_solution(17666814842247780693)
XLA Ops:
  0.7 2.1 slice_bitcast_fusion.7
  2.7 2.4 collective-permute-start
  5.1 2.5 slice_bitcast_fusion.6
  7.7 2.4 collective-permute-start.7
  10.1 1.9 collective-permute-start.5
  12.1 2.1 collective-permute-start.3
  15.6 1.9 collective-permute-start.1
  17.9 1.7 convolution_bitcast_fusion
  19.6 1.7 fusion.8
  21.3 30.8 %collective-permute-done.3.lower = f32[2,256,256]{2,1,0:T(8,128)S(1)} collective-permute-done((f32[2,256,256]{2,1,0:T(8,128)S(1)}, f32[2,256,256]{2,1,0:T(8,128)S(1)}, u32[]{:S(2)}, u32[]{:S(2)}) %collective-permute-start.3) | collective-permute-done | bytes 524320 | tf_op jit(solution)/shard_map/ppermute | solution.py:22
  53.5 1.9 collective-permute-start.4
  57.6 2.4 collective-permute-start.2
  60.0 1.8 fusion.10
  62.9 1.9 collective-permute-start.8
  66.0 2.3 collective-permute-start.6
  68.4 10.9 %collective-permute-done.2.refs_1_ = f32[2,256,256]{2,1,0:T(8,128)} collective-permute-done((f32[2,256,256]{2,1,0:T(8,128)}, f32[2,256,256]{2,1,0:T(8,128)}, u32[]{:S(2)}, u32[]{:S(2)}) %collective-permute-start.2) | collective-permute-done | bytes 524320 | tf_op jit(solution)/shard_map/ppermute | solution.py:22
  79.2 9.3 %forward.3 = (f32[3,2,256,256]{3,2,1,0:T(8,128)}, f32[3,2,256,256]{3,2,1,0:T(8,128)}) custom-call(s32[3,2]{1,0:T(4,128)} %copy.17.pos, f32[4,2,512,256]{3,2,1,0:T(8,128)} %own.7, f32[2,256,256]{2,1,0:T(8,128)} %collective-permute-done.lower, f32[2,512,256]{2,1,0:T(8,128)} %collective-permute-done.1.refs_0_, f32[2,256,256]{2,1,0:T(8,128)} %collective-permute-done.2.refs_1_, ...), custom_call_target="tpu_custom_call" | custom-call | flops 10000000000 | bytes 12582912 | tf_op jit(solution)/shard_map/forward/pallas_call | solution.py:269
  88.5 9.3 %forward.4 = (f32[3,2,256,256]{3,2,1,0:T(8,128)}, f32[3,2,256,256]{3,2,1,0:T(8,128)}) custom-call(s32[3,2]{1,0:T(4,128)} %copy.17.pos, f32[4,2,512,256]{3,2,1,0:T(8,128)} %own.7, f32[2,256,256]{2,1,0:T(8,128)} %copy-done.14, f32[2,768,256]{2,1,0:T(8,128)} %collective-permute-done.4.refs_0_, f32[3,2,256,256]{3,2,1,0:T(8,128)} %get-tuple-element.76.refs_1_.wave, ...), custom_call_target="tpu_custom_call" | custom-call | flops 10000000000 | bytes 12582912 | tf_op jit(solution)/shard_map/forward/pallas_call | solution.py:269
  97.9 15.0 %collective-permute-done.6.refs_0_ = f32[2,768,256]{2,1,0:T(8,128)S(1)} collective-permute-done((f32[2,768,256]{2,1,0:T(8,128)S(1)}, f32[2,768,256]{2,1,0:T(8,128)S(1)}, u32[]{:S(2)}, u32[]{:S(2)}) %collective-permute-start.6) | collective-permute-done | bytes 1572896 | tf_op jit(solution)/shard_map/ppermute | solution.py:22
  114.0 9.2 %forward.5 = (f32[3,2,256,256]{3,2,1,0:T(8,128)}, f32[3,2,256,256]{3,2,1,0:T(8,128)}) custom-call(s32[3,2]{1,0:T(4,128)} %copy.17.pos, f32[4,2,512,256]{3,2,1,0:T(8,128)} %own.7, f32[2,256,256]{2,1,0:T(8,128)} %collective-permute-done.5.lower, f32[2,768,256]{2,1,0:T(8,128)} %copy-done.18, f32[3,2,256,256]{3,2,1,0:T(8,128)} %get-tuple-element.78.refs_1_.wave, ...), custom_call_target="tpu_custom_call" | custom-call | flops 10000000000 | bytes 12582912 | tf_op jit(solution)/shard_map/forward/pallas_call | solution.py:269
  124.4 11.3 %turn.1 = (f32[2,512,256]{2,1,0:T(8,128)}, f32[2,256,256]{2,1,0:T(8,128)}, f32[2,768,256]{2,1,0:T(8,128)}, f32[3,2,256,256]{3,2,1,0:T(8,128)}) custom-call(s32[3,2]{1,0:T(4,128)} %copy.17.pos, s32[1]{0:T(128)S(6)} %copy.28.count, f32[4,2,512,256]{3,2,1,0:T(8,128)} %own.7, f32[2,256,256]{2,1,0:T(8,128)} %collective-permute-done.7.lower, ...), custom_call_target="tpu_custom_call" | custom-call | flops 10000000000 | bytes 12582912 | tf_op jit(solution)/shard_map/turn/pallas_call | solution.py:288
  135.7 10.2 %backward.3 = (f32[2,512,256]{2,1,0:T(8,128)}, f32[2,256,256]{2,1,0:T(8,128)}, f32[2,768,256]{2,1,0:T(8,128)}, f32[3,2,256,256]{3,2,1,0:T(8,128)}) custom-call(s32[3,2]{1,0:T(4,128)} %copy.17.pos, f32[3,2,256,256]{3,2,1,0:T(8,128)} %get-tuple-element.79.slab, f32[3,2,256,256]{3,2,1,0:T(8,128)} %get-tuple-element.78.refs_1_.wave, ...), custom_call_target="tpu_custom_call" | custom-call | flops 10000000000 | bytes 12582912 | tf_op jit(solution)/shard_map/backward/pallas_call | solution.py:308
  145.9 10.3 %backward.4 = (f32[2,512,256]{2,1,0:T(8,128)}, f32[2,256,256]{2,1,0:T(8,128)}, f32[2,768,256]{2,1,0:T(8,128)}, f32[3,2,256,256]{3,2,1,0:T(8,128)}) custom-call(s32[3,2]{1,0:T(4,128)} %copy.17.pos, f32[3,2,256,256]{3,2,1,0:T(8,128)} %get-tuple-element.77.slab, f32[3,2,256,256]{3,2,1,0:T(8,128)} %get-tuple-element.76.refs_1_.wave, ...), custom_call_target="tpu_custom_call" | custom-call | flops 10000000000 | bytes 12582912 | tf_op jit(solution)/shard_map/backward/pallas_call | solution.py:308
  156.2 10.1 %backward.5 = (f32[2,512,256]{2,1,0:T(8,128)}, f32[2,256,256]{2,1,0:T(8,128)}, f32[2,512,256]{2,1,0:T(8,128)}, f32[2,256,256]{2,1,0:T(8,128)}, f32[1,2,256,256]{3,2,1,0:T(8,128)}) custom-call(s32[3,2]{1,0:T(4,128)} %copy.17.pos, f32[3,2,256,256]{3,2,1,0:T(8,128)} %get-tuple-element.75.slab, f32[1,2,256,256]{3,2,1,0:T(8,128)} %bitcast.70, ...), custom_call_target="tpu_custom_call" | custom-call | flops 10000000000 | bytes 12582912 | tf_op jit(solution)/shard_map/backward/pallas_call | solution.py:308
  167.2 3.1 %collective-permute-start.18 = (f32[256,256]{1,0:T(8,128)S(1)}, f32[256,256]{1,0:T(8,128)S(1)}, u32[]{:S(2)}, u32[]{:S(2)}) collective-permute-start(f32[256,256]{1,0:T(8,128)S(1)} %constant_dynamic-slice_fusion.3), channel_id=1, source_target_pairs={{0,1},{1,0},{2,3},{3,2},{4,5},{5,4},{6,7},{7,6},{8,9},{9,8},{10,11... | collective-permute-start | bytes 786440 | tf_op jit(solution)/shard_map/ppermute | solution.py:348
  173.0 3.2 %collective-permute-start.20 = (f32[64,256]{1,0:T(8,128)S(1)}, f32[64,256]{1,0:T(8,128)S(1)}, u32[]{:S(2)}, u32[]{:S(2)}) collective-permute-start(f32[64,256]{1,0:T(8,128)S(1)} %get-tuple-element.109), channel_id=1, source_target_pairs={{0,16},{1,17},{2,18},{3,19},{4,20},{5,21},{6,22},{7,23},{8,24},{9,... | collective-permute-start | bytes 196616 | tf_op jit(solution)/shard_map/ppermute | solution.py:348
  177.2 1.5 collective-permute-done.20
  178.7 2.9 collective-permute-done.19
  184.8 1.9 collective-permute-start.16
  186.7 1.9 collective-permute-start.10
  188.7 2.2 collective-permute-start.27
  194.3 1.9 collective-permute-start.9
  197.4 26.6 %collective-permute-start.28 = (f32[64,256]{1,0:T(8,128)S(1)}, f32[64,256]{1,0:T(8,128)S(1)}, u32[]{:S(2)}, u32[]{:S(2)}) collective-permute-start(f32[64,256]{1,0:T(8,128)S(1)} %get-tuple-element.99), channel_id=1, source_target_pairs={{0,8},{1,9},{2,10},{3,11},{4,12},{5,13},{6,14},{7,15},{8,16},{9,17... | collective-permute-start | bytes 196616 | tf_op jit(solution)/shard_map/ppermute | solution.py:348
  224.0 1.9 collective-permute-start.14
  225.9 1.9 collective-permute-done.28
  227.9 2.5 collective-permute-start.29
  231.1 2.1 add.160
  233.9 3.8 %collective-permute-start.11 = (f32[2,256,256]{2,1,0:T(8,128)}, f32[2,256,256]{2,1,0:T(8,128)}, u32[]{:S(2)}, u32[]{:S(2)}) collective-permute-start(f32[2,256,256]{2,1,0:T(8,128)} %add.160), channel_id=1, source_target_pairs={{0,32},{32,64},{64,96},{1,33},{33,65},{65,97},{2,34},{34,66},{66,9... | collective-permute-start | bytes 1572872 | tf_op jit(solution)/shard_map/ppermute | solution.py:22
  237.8 16.9 %collective-permute-start.31 = (f32[256,256]{1,0:T(8,128)S(1)}, f32[256,256]{1,0:T(8,128)}, u32[]{:S(2)}, u32[]{:S(2)}) collective-permute-start(f32[256,256]{1,0:T(8,128)S(1)} %constant_dynamic-update-slice_fusion.2), channel_id=1, source_target_pairs={{0,1},{1,0},{2,3},{3,2},{4,5},{5,4},{6,7},{7,6},{8,9},{9,8},{10,11... | collective-permute-start | bytes 786440 | tf_op jit(solution)/shard_map/ppermute | solution.py:348
  256.0 2.3 collective-permute-start.12
  259.4 1.5 add.159
  263.6 1.9 collective-permute-start.17
  266.8 1.9 collective-permute-start.15
  268.7 9.2 %collective-permute-done.12 = f32[2,768,256]{2,1,0:T(8,128)S(1)} collective-permute-done((f32[2,768,256]{2,1,0:T(8,128)}, f32[2,768,256]{2,1,0:T(8,128)S(1)}, u32[]{:S(2)}, u32[]{:S(2)}) %collective-permute-start.12) | collective-permute-done | bytes 1572896 | tf_op jit(solution)/shard_map/ppermute | solution.py:22
  279.2 1.9 collective-permute-start.13
  281.2 10.3 %collective-permute-done.15 = f32[2,256,256]{2,1,0:T(8,128)S(1)} collective-permute-done((f32[2,256,256]{2,1,0:T(8,128)S(1)}, f32[2,256,256]{2,1,0:T(8,128)S(1)}, u32[]{:S(2)}, u32[]{:S(2)}) %collective-permute-start.15) | collective-permute-done | bytes 524320 | tf_op jit(solution)/shard_map/ppermute | solution.py:22
  291.6 10.5 %collective-permute-done.13 = f32[2,256,256]{2,1,0:T(8,128)S(1)} collective-permute-done((f32[2,256,256]{2,1,0:T(8,128)S(1)}, f32[2,256,256]{2,1,0:T(8,128)S(1)}, u32[]{:S(2)}, u32[]{:S(2)}) %collective-permute-start.13) | collective-permute-done | bytes 524320 | tf_op jit(solution)/shard_map/ppermute | solution.py:22
  302.1 2.5 pad_maximum_fusion
  (103 shorter events, 30.7 us)
Async XLA Ops:
  0.6 17.3 %copy-start = (f32[3,256,256]{2,1,0:T(8,128)S(1)}, f32[3,256,256]{2,1,0:T(8,128)}, u32[]{:S(2)}) copy-start(f32[3,256,256]{2,1,0:T(8,128)} %param.22) | copy-start | bytes 2359300
  0.6 13.5 %copy-start.2 = (f32[4,2,512,256]{3,2,1,0:T(8,128)S(1)}, f32[4,2,512,256]{3,2,1,0:T(8,128)}, u32[]{:S(2)}) copy-start(f32[4,2,512,256]{3,2,1,0:T(8,128)} %own.7) | copy-start | bytes 12582916
  2.7 54.9 %collective-permute-start = (f32[2,256,256]{2,1,0:T(8,128)}, f32[2,256,256]{2,1,0:T(8,128)}, u32[]{:S(2)}, u32[]{:S(2)}) collective-permute-start(f32[2,256,256]{2,1,0:T(8,128)} %slice_bitcast_fusion.7), channel_id=1, source_target_pairs={{32,0},{64,32},{96,64},{33,1},{65,33},{97,65},{34,2},{66,34},{98,6... | collective-permute-start | bytes 1572872 | tf_op jit(solution)/shard_map/ppermute | solution.py:22
  7.7 54.1 %collective-permute-start.7 = (f32[2,256,256]{2,1,0:T(8,128)}, f32[2,256,256]{2,1,0:T(8,128)}, u32[]{:S(2)}, u32[]{:S(2)}) collective-permute-start(f32[2,256,256]{2,1,0:T(8,128)} %get-tuple-element.105), channel_id=1, source_target_pairs={{32,0},{64,32},{96,64},{33,1},{65,33},{97,65},{34,2},{66,34},{98,6... | collective-permute-start | bytes 1572872 | tf_op jit(solution)/shard_map/ppermute | solution.py:22
  10.1 54.8 %collective-permute-start.5 = (f32[2,256,256]{2,1,0:T(8,128)}, f32[2,256,256]{2,1,0:T(8,128)}, u32[]{:S(2)}, u32[]{:S(2)}) collective-permute-start(f32[2,256,256]{2,1,0:T(8,128)} %get-tuple-element.106), channel_id=1, source_target_pairs={{32,0},{64,32},{96,64},{33,1},{65,33},{97,65},{34,2},{66,34},{98,6... | collective-permute-start | bytes 1572872 | tf_op jit(solution)/shard_map/ppermute | solution.py:22
  12.0 5.4 %copy-start.9 = (f32[256,256]{1,0:T(8,128)S(1)}, f32[256,256]{1,0:T(8,128)}, u32[]{:S(2)}) copy-start(f32[256,256]{1,0:T(8,128)} %constant.181.clone) | copy-start | bytes 786436
  12.0 5.4 %copy-start.15 = (f32[256,256]{1,0:T(8,128)S(1)}, f32[256,256]{1,0:T(8,128)}, u32[]{:S(2)}) copy-start(f32[256,256]{1,0:T(8,128)} %param.19) | copy-start | bytes 786436
  12.1 5.9 %copy-start.8 = (f32[256,256,1]{1,0,2:T(8,128)S(1)}, f32[256,256,1]{1,0,2:T(8,128)}, u32[]{:S(2)}) copy-start(f32[256,256,1]{1,0,2:T(8,128)} %constant.185) | copy-start | bytes 786436
  12.1 40.1 %collective-permute-start.3 = (f32[2,256,256]{2,1,0:T(8,128)S(1)}, f32[2,256,256]{2,1,0:T(8,128)S(1)}, u32[]{:S(2)}, u32[]{:S(2)}) collective-permute-start(f32[2,256,256]{2,1,0:T(8,128)S(1)} %get-tuple-element.104), channel_id=1, source_target_pairs={{32,0},{64,32},{96,64},{33,1},{65,33},{97,65},{34,2},{66,34},{98,6... | collective-permute-start | bytes 1572872 | tf_op jit(solution)/shard_map/ppermute | solution.py:22
  15.6 52.8 %collective-permute-start.1 = (f32[2,512,256]{2,1,0:T(8,128)}, f32[2,512,256]{2,1,0:T(8,128)}, u32[]{:S(2)}, u32[]{:S(2)}) collective-permute-start(f32[2,512,256]{2,1,0:T(8,128)} %get-tuple-element.100), channel_id=1, source_target_pairs={{1,0},{2,1},{3,2},{4,3},{5,4},{6,5},{7,6},{8,7},{9,8},{10,9},{11,1... | collective-permute-start | bytes 3145736 | tf_op jit(solution)/shard_map/ppermute | solution.py:22
  52.2 1.3 copy-start.14
  52.2 4.1 %copy-start.16 = (s32[3,2]{0,1:T(2,128)S(1)}, s32[3,2]{0,1:T(2,128)}, u32[]{:S(2)}) copy-start(s32[3,2]{0,1:T(2,128)} %param.20) | copy-start | bytes 76
  52.2 7.9 %copy-start.3 = (f32[3,256,256]{2,1,0:T(8,128)S(1)}, f32[3,256,256]{2,1,0:T(8,128)}, u32[]{:S(2)}) copy-start(f32[3,256,256]{2,1,0:T(8,128)} %convolution_bitcast_fusion) | copy-start | bytes 2359300
  53.5 35.1 %collective-permute-start.4 = (f32[2,768,256]{2,1,0:T(8,128)}, f32[2,768,256]{2,1,0:T(8,128)}, u32[]{:S(2)}, u32[]{:S(2)}) collective-permute-start(f32[2,768,256]{2,1,0:T(8,128)} %pad_maximum_fusion.1), channel_id=1, source_target_pairs={{1,0},{2,1},{3,2},{4,3},{5,4},{6,5},{7,6},{8,7},{9,8},{10,9},{11,1... | collective-permute-start | bytes 4718600 | tf_op jit(solution)/shard_map/ppermute | solution.py:22
  57.6 21.6 %collective-permute-start.2 = (f32[2,256,256]{2,1,0:T(8,128)}, f32[2,256,256]{2,1,0:T(8,128)}, u32[]{:S(2)}, u32[]{:S(2)}) collective-permute-start(f32[2,256,256]{2,1,0:T(8,128)} %collective-permute-done.lower), channel_id=1, source_target_pairs={{1,0},{2,1},{3,2},{4,3},{5,4},{6,5},{7,6},{8,7},{9,8},{10,9},{11,1... | collective-permute-start | bytes 1572872 | tf_op jit(solution)/shard_map/ppermute | solution.py:22
  62.9 60.3 %collective-permute-start.8 = (f32[2,768,256]{2,1,0:T(8,128)S(1)}, f32[2,768,256]{2,1,0:T(8,128)S(1)}, u32[]{:S(2)}, u32[]{:S(2)}) collective-permute-start(f32[2,768,256]{2,1,0:T(8,128)S(1)} %pad_maximum_fusion.3), channel_id=1, source_target_pairs={{1,0},{2,1},{3,2},{4,3},{5,4},{6,5},{7,6},{8,7},{9,8},{10,9},{11,1... | collective-permute-start | bytes 4718600 | tf_op jit(solution)/shard_map/ppermute | solution.py:22
  66.0 46.8 %collective-permute-start.6 = (f32[2,768,256]{2,1,0:T(8,128)S(1)}, f32[2,768,256]{2,1,0:T(8,128)S(1)}, u32[]{:S(2)}, u32[]{:S(2)}) collective-permute-start(f32[2,768,256]{2,1,0:T(8,128)S(1)} %pad_maximum_fusion.2), channel_id=1, source_target_pairs={{1,0},{2,1},{3,2},{4,3},{5,4},{6,5},{7,6},{8,7},{9,8},{10,9},{11,1... | collective-permute-start | bytes 4718600 | tf_op jit(solution)/shard_map/ppermute | solution.py:22
  112.8 1.1 copy-start.18
  123.2 1.1 copy-start.17
  167.2 4.2 %collective-permute-start.18 = (f32[256,256]{1,0:T(8,128)S(1)}, f32[256,256]{1,0:T(8,128)S(1)}, u32[]{:S(2)}, u32[]{:S(2)}) collective-permute-start(f32[256,256]{1,0:T(8,128)S(1)} %constant_dynamic-slice_fusion.3), channel_id=1, source_target_pairs={{0,1},{1,0},{2,3},{3,2},{4,5},{5,4},{6,7},{7,6},{8,9},{9,8},{10,11... | collective-permute-start | bytes 786440 | tf_op jit(solution)/shard_map/ppermute | solution.py:348
  172.5 4.7 %collective-permute-start.21 = (f32[64,256]{1,0:T(8,128)S(1)}, f32[64,256]{1,0:T(8,128)S(1)}, u32[]{:S(2)}, u32[]{:S(2)}) collective-permute-start(f32[64,256]{1,0:T(8,128)S(1)} %get-tuple-element.108), channel_id=1, source_target_pairs={{0,24},{1,25},{2,26},{3,27},{4,28},{5,29},{6,30},{7,31},{8,0},{9,1... | collective-permute-start | bytes 196616 | tf_op jit(solution)/shard_map/ppermute | solution.py:348
  173.0 5.8 %collective-permute-start.20 = (f32[64,256]{1,0:T(8,128)S(1)}, f32[64,256]{1,0:T(8,128)S(1)}, u32[]{:S(2)}, u32[]{:S(2)}) collective-permute-start(f32[64,256]{1,0:T(8,128)S(1)} %get-tuple-element.109), channel_id=1, source_target_pairs={{0,16},{1,17},{2,18},{3,19},{4,20},{5,21},{6,22},{7,23},{8,24},{9,... | collective-permute-start | bytes 196616 | tf_op jit(solution)/shard_map/ppermute | solution.py:348
  176.2 5.5 %collective-permute-start.19 = (f32[64,256]{1,0:T(8,128)S(1)}, f32[64,256]{1,0:T(8,128)S(1)}, u32[]{:S(2)}, u32[]{:S(2)}) collective-permute-start(f32[64,256]{1,0:T(8,128)S(1)} %get-tuple-element.107), channel_id=1, source_target_pairs={{0,8},{1,9},{2,10},{3,11},{4,12},{5,13},{6,14},{7,15},{8,16},{9,17... | collective-permute-start | bytes 196616 | tf_op jit(solution)/shard_map/ppermute | solution.py:348
  181.7 7.0 %collective-permute-start.24 = (f32[64,256]{1,0:T(8,128)S(1)}, f32[64,256]{1,0:T(8,128)S(1)}, u32[]{:S(2)}, u32[]{:S(2)}) collective-permute-start(f32[64,256]{1,0:T(8,128)S(1)} %add_add_fusion.2), channel_id=1, source_target_pairs={{0,96},{1,97},{2,98},{3,99},{4,100},{5,101},{6,102},{7,103},{8,104... | collective-permute-start | bytes 196616 | tf_op jit(solution)/shard_map/ppermute | solution.py:348
  182.3 6.4 %collective-permute-start.23 = (f32[64,256]{1,0:T(8,128)S(1)}, f32[64,256]{1,0:T(8,128)S(1)}, u32[]{:S(2)}, u32[]{:S(2)}) collective-permute-start(f32[64,256]{1,0:T(8,128)S(1)} %add_add_fusion.2), channel_id=1, source_target_pairs={{0,64},{1,65},{2,66},{3,67},{4,68},{5,69},{6,70},{7,71},{8,72},{9,... | collective-permute-start | bytes 196616 | tf_op jit(solution)/shard_map/ppermute | solution.py:348
  183.4 5.3 %collective-permute-start.22 = (f32[64,256]{1,0:T(8,128)S(1)}, f32[64,256]{1,0:T(8,128)S(1)}, u32[]{:S(2)}, u32[]{:S(2)}) collective-permute-start(f32[64,256]{1,0:T(8,128)S(1)} %add_add_fusion.2), channel_id=1, source_target_pairs={{0,32},{1,33},{2,34},{3,35},{4,36},{5,37},{6,38},{7,39},{8,40},{9,... | collective-permute-start | bytes 196616 | tf_op jit(solution)/shard_map/ppermute | solution.py:348
  184.8 77.4 %collective-permute-start.16 = (f32[2,768,256]{2,1,0:T(8,128)}, f32[2,768,256]{2,1,0:T(8,128)S(1)}, u32[]{:S(2)}, u32[]{:S(2)}) collective-permute-start(f32[2,768,256]{2,1,0:T(8,128)} %get-tuple-element.95), channel_id=1, source_target_pairs={{0,1},{1,2},{2,3},{3,4},{4,5},{5,6},{6,7},{7,8},{8,9},{9,10},{10,1... | collective-permute-start | bytes 4718600 | tf_op jit(solution)/shard_map/ppermute | solution.py:22
  186.7 43.6 %collective-permute-start.10 = (f32[2,256,256]{2,1,0:T(8,128)}, f32[2,256,256]{2,1,0:T(8,128)}, u32[]{:S(2)}, u32[]{:S(2)}) collective-permute-start(f32[2,256,256]{2,1,0:T(8,128)} %get-tuple-element.87), channel_id=1, source_target_pairs={{0,1},{1,2},{2,3},{3,4},{4,5},{5,6},{6,7},{7,8},{8,9},{9,10},{10,1... | collective-permute-start | bytes 1572872 | tf_op jit(solution)/shard_map/ppermute | solution.py:22
  188.7 5.5 %collective-permute-start.27 = (f32[64,256]{1,0:T(8,128)S(1)}, f32[64,256]{1,0:T(8,128)S(1)}, u32[]{:S(2)}, u32[]{:S(2)}) collective-permute-start(f32[64,256]{1,0:T(8,128)S(1)} %add_add_fusion.1), channel_id=1, source_target_pairs={{0,6},{1,7},{2,0},{3,1},{4,2},{5,3},{6,4},{7,5},{8,14},{9,15},{10,... | collective-permute-start | bytes 196616 | tf_op jit(solution)/shard_map/ppermute | solution.py:348
  190.9 5.8 %collective-permute-start.26 = (f32[64,256]{1,0:T(8,128)S(1)}, f32[64,256]{1,0:T(8,128)S(1)}, u32[]{:S(2)}, u32[]{:S(2)}) collective-permute-start(f32[64,256]{1,0:T(8,128)S(1)} %add_add_fusion.1), channel_id=1, source_target_pairs={{0,4},{1,5},{2,6},{3,7},{4,0},{5,1},{6,2},{7,3},{8,12},{9,13},{10,... | collective-permute-start | bytes 196616 | tf_op jit(solution)/shard_map/ppermute | solution.py:348
  192.4 5.0 %collective-permute-start.25 = (f32[64,256]{1,0:T(8,128)S(1)}, f32[64,256]{1,0:T(8,128)S(1)}, u32[]{:S(2)}, u32[]{:S(2)}) collective-permute-start(f32[64,256]{1,0:T(8,128)S(1)} %add_add_fusion.1), channel_id=1, source_target_pairs={{0,2},{1,3},{2,4},{3,5},{4,6},{5,7},{6,0},{7,1},{8,10},{9,11},{10,... | collective-permute-start | bytes 196616 | tf_op jit(solution)/shard_map/ppermute | solution.py:348
  194.3 65.1 %collective-permute-start.9 = (f32[2,512,256]{2,1,0:T(8,128)}, f32[2,512,256]{2,1,0:T(8,128)}, u32[]{:S(2)}, u32[]{:S(2)}) collective-permute-start(f32[2,512,256]{2,1,0:T(8,128)} %get-tuple-element.85), channel_id=1, source_target_pairs={{0,1},{1,2},{2,3},{3,4},{4,5},{5,6},{6,7},{7,8},{8,9},{9,10},{10,1... | collective-permute-start | bytes 3145736 | tf_op jit(solution)/shard_map/ppermute | solution.py:22
  197.4 30.5 %collective-permute-start.28 = (f32[64,256]{1,0:T(8,128)S(1)}, f32[64,256]{1,0:T(8,128)S(1)}, u32[]{:S(2)}, u32[]{:S(2)}) collective-permute-start(f32[64,256]{1,0:T(8,128)S(1)} %get-tuple-element.99), channel_id=1, source_target_pairs={{0,8},{1,9},{2,10},{3,11},{4,12},{5,13},{6,14},{7,15},{8,16},{9,17... | collective-permute-start | bytes 196616 | tf_op jit(solution)/shard_map/ppermute | solution.py:348
  224.0 41.5 %collective-permute-start.14 = (f32[2,768,256]{2,1,0:T(8,128)}, f32[2,768,256]{2,1,0:T(8,128)S(1)}, u32[]{:S(2)}, u32[]{:S(2)}) collective-permute-start(f32[2,768,256]{2,1,0:T(8,128)} %get-tuple-element.92), channel_id=1, source_target_pairs={{0,1},{1,2},{2,3},{3,4},{4,5},{5,6},{6,7},{7,8},{8,9},{9,10},{10,1... | collective-permute-start | bytes 4718600 | tf_op jit(solution)/shard_map/ppermute | solution.py:22
  227.9 6.0 %collective-permute-start.29 = (f32[64,256]{1,0:T(8,128)S(1)}, f32[64,256]{1,0:T(8,128)S(1)}, u32[]{:S(2)}, u32[]{:S(2)}) collective-permute-start(f32[64,256]{1,0:T(8,128)S(1)} %get-tuple-element.99), channel_id=1, source_target_pairs={{0,16},{1,17},{2,18},{3,19},{4,20},{5,21},{6,22},{7,23},{8,24},{9,... | collective-permute-start | bytes 196616 | tf_op jit(solution)/shard_map/ppermute | solution.py:348
  230.4 7.4 %collective-permute-start.30 = (f32[64,256]{1,0:T(8,128)S(1)}, f32[64,256]{1,0:T(8,128)S(1)}, u32[]{:S(2)}, u32[]{:S(2)}) collective-permute-start(f32[64,256]{1,0:T(8,128)S(1)} %get-tuple-element.99), channel_id=1, source_target_pairs={{0,24},{1,25},{2,26},{3,27},{4,28},{5,29},{6,30},{7,31},{8,0},{9,1... | collective-permute-start | bytes 196616 | tf_op jit(solution)/shard_map/ppermute | solution.py:348
  233.9 27.1 %collective-permute-start.11 = (f32[2,256,256]{2,1,0:T(8,128)}, f32[2,256,256]{2,1,0:T(8,128)}, u32[]{:S(2)}, u32[]{:S(2)}) collective-permute-start(f32[2,256,256]{2,1,0:T(8,128)} %add.160), channel_id=1, source_target_pairs={{0,32},{32,64},{64,96},{1,33},{33,65},{65,97},{2,34},{34,66},{66,9... | collective-permute-start | bytes 1572872 | tf_op jit(solution)/shard_map/ppermute | solution.py:22
  237.8 18.2 %collective-permute-start.31 = (f32[256,256]{1,0:T(8,128)S(1)}, f32[256,256]{1,0:T(8,128)}, u32[]{:S(2)}, u32[]{:S(2)}) collective-permute-start(f32[256,256]{1,0:T(8,128)S(1)} %constant_dynamic-update-slice_fusion.2), channel_id=1, source_target_pairs={{0,1},{1,0},{2,3},{3,2},{4,5},{5,4},{6,7},{7,6},{8,9},{9,8},{10,11... | collective-permute-start | bytes 786440 | tf_op jit(solution)/shard_map/ppermute | solution.py:348
  254.7 4.7 %copy-start.7 = (f32[2,512,256]{2,1,0:T(8,128)S(1)}, f32[2,512,256]{2,1,0:T(8,128)}, u32[]{:S(2)}) copy-start(f32[2,512,256]{2,1,0:T(8,128)} %get-tuple-element.84) | copy-start | bytes 3145732
  256.0 21.9 %collective-permute-start.12 = (f32[2,768,256]{2,1,0:T(8,128)}, f32[2,768,256]{2,1,0:T(8,128)S(1)}, u32[]{:S(2)}, u32[]{:S(2)}) collective-permute-start(f32[2,768,256]{2,1,0:T(8,128)} %get-tuple-element.89), channel_id=1, source_target_pairs={{0,1},{1,2},{2,3},{3,4},{4,5},{5,6},{6,7},{7,8},{8,9},{9,10},{10,1... | collective-permute-start | bytes 4718600 | tf_op jit(solution)/shard_map/ppermute | solution.py:22
  259.3 1.6 copy-start.13
  260.9 1.4 copy-start.6
  262.5 3.0 copy-start.5
  263.6 17.6 %collective-permute-start.17 = (f32[2,256,256]{2,1,0:T(8,128)S(1)}, f32[2,256,256]{2,1,0:T(8,128)S(1)}, u32[]{:S(2)}, u32[]{:S(2)}) collective-permute-start(f32[2,256,256]{2,1,0:T(8,128)S(1)} %slice_add_fusion.3), channel_id=1, source_target_pairs={{0,32},{32,64},{64,96},{1,33},{33,65},{65,97},{2,34},{34,66},{66,9... | collective-permute-start | bytes 1572872 | tf_op jit(solution)/shard_map/ppermute | solution.py:22
  265.7 12.3 %copy-start.4 = (f32[2,512,256]{2,1,0:T(8,128)S(1)}, f32[2,512,256]{2,1,0:T(8,128)}, u32[]{:S(2)}) copy-start(f32[2,512,256]{2,1,0:T(8,128)} %get-tuple-element.88) | copy-start | bytes 3145732
  266.8 24.7 %collective-permute-start.15 = (f32[2,256,256]{2,1,0:T(8,128)S(1)}, f32[2,256,256]{2,1,0:T(8,128)S(1)}, u32[]{:S(2)}, u32[]{:S(2)}) collective-permute-start(f32[2,256,256]{2,1,0:T(8,128)S(1)} %slice_add_fusion.5), channel_id=1, source_target_pairs={{0,32},{32,64},{64,96},{1,33},{33,65},{65,97},{2,34},{34,66},{66,9... | collective-permute-start | bytes 1572872 | tf_op jit(solution)/shard_map/ppermute | solution.py:22
  279.2 22.8 %collective-permute-start.13 = (f32[2,256,256]{2,1,0:T(8,128)S(1)}, f32[2,256,256]{2,1,0:T(8,128)S(1)}, u32[]{:S(2)}, u32[]{:S(2)}) collective-permute-start(f32[2,256,256]{2,1,0:T(8,128)S(1)} %slice_add_fusion.7), channel_id=1, source_target_pairs={{0,32},{32,64},{64,96},{1,33},{33,65},{65,97},{2,34},{34,66},{66,9... | collective-permute-start | bytes 1572872 | tf_op jit(solution)/shard_map/ppermute | solution.py:22
  302.1 2.5 copy-start.1
  (3 other events, 3.1 us)
where the time goes:
time: 306 us; the launch traced here: 305 us
  starting transfers between devices  101 us (33%)
  waiting for transfers between devices  98 us (32%)
  Pallas kernels  69.7 us (23%)
  local copies, waits for them, and re-layouts  14.4 us (5%)
  other arithmetic  13.5 us (4%)
  matrix products  5.56 us (2%)
    ppermute x18, waiting for transfers between devices, shift(): return lax.ppermute(x, axis, pairs)  86.7 us
    ppermute x14, starting transfers between devices, turn_by(): return lax.ppermute(x, ('row', 'col'), pairs)  62.6 us
    ppermute x18, starting transfers between devices, shift(): return lax.ppermute(x, axis, pairs)  38.8 us
    pallas_call x3, Pallas kernels, run_backward(): pl.pallas_call(functools.partial(backward_kernel, first), grid_spec=pltpu...  30.6 us
    pallas_call x3, Pallas kernels, run_forward(): pl.pallas_call(functools.partial(forward_kernel, len(sides)), grid_spec=p...  27.9 us
    ppermute x14, waiting for transfers between devices, turn_by(): return lax.ppermute(x, ('row', 'col'), pairs)  11.3 us
    pallas_call x1, Pallas kernels, run_turn(): pl.pallas_call(functools.partial(turn_kernel, len(sides)), grid_spec=pltp...  11.3 us
    unnamed x43, local copies, waits for them, and re-layouts  6.31 us
  transfers between devices with their start and end apart: 32, of which 15 were waited for; matrix products, arithmetic and copies ran while one was open for 7% of the time, Pallas kernels for 9%

commit v1 on v0

--- a/solution.py
+++ b/solution.py
@@ -29,12 +29,12 @@
     tables = []
     for angle in (even, odd):
         cos, sin = np.cos(angle) / 16.0, np.sin(angle) / 16.0
-        table = np.block([[cos, -sin], [sin, cos]])
-        tables += [table, table.T]
+        tables.append(np.block([[cos, -sin], [sin, cos]]))
     whole = np.stack(tables).astype(np.float32)
     high = whole.astype(jnp.bfloat16)
     low = (whole - high.astype(np.float32)).astype(jnp.bfloat16)
-    return np.stack([high, low], axis=1)
+    held = lax.optimization_barrier(jnp.asarray(np.stack([high, low], axis=1)))
+    return jnp.stack([held, held.transpose(0, 1, 3, 2)], axis=1).reshape(4, 2, WIN, WIN)
 
 
 def split(x):
@@ -250,7 +250,7 @@
 TILE = (2, 512, 256)
 STRIP = (2, 256, 256)
 SIDE = (2, 768, 256)
-PARAMS = pltpu.CompilerParams(dimension_semantics=("arbitrary",), vmem_limit_bytes=56 << 20)
+PARAMS = pltpu.CompilerParams(dimension_semantics=("arbitrary",), vmem_limit_bytes=26 << 20)
 COST = pl.CostEstimate(flops=10 * 1000 * 1000 * 1000, bytes_accessed=12 << 20, transcendentals=0)
 EXT = pltpu.VMEM((2, 4, 768, HALF), F32)
 TABLES = (4, 2, 256, 256)
@@ -325,58 +325,53 @@
 
 
 def parity_order(x):
-    order = np.concatenate([np.arange(0, WIN, 2), np.arange(1, WIN, 2)])
-    pick = jnp.asarray(np.eye(WIN, dtype=np.float32)[order])
+    place = lax.broadcasted_iota(jnp.int32, (WIN, WIN), 0)
+    source = lax.broadcasted_iota(jnp.int32, (WIN, WIN), 1)
+    pick = (source == place % HALF * 2 + place // HALF).astype(F32)
     high = lax.Precision.HIGHEST
     x = jnp.einsum("...rc,dc->...rd", x, pick, precision=high)
     return jnp.einsum("er,...rd->...ed", pick, x, precision=high)
 
 
-def turn_by(x, axis, by):
-    sizes = {"x": lax.axis_size("row"), "y": 4, "z": 4, "core": 2}
-    pairs = []
-    for x_at in range(sizes["x"]):
-        for y_at in range(4):
-            for z_at in range(4):
-                for core in range(2):
-                    place = {"x": x_at, "y": y_at, "z": z_at, "core": core}
-                    there = dict(place)
-                    there[axis] = (place[axis] + by) % sizes[axis]
-                    pairs.append(tuple(
-                        p["x"] * 32 + p["y"] * 8 + p["z"] * 2 + p["core"] for p in (place, there)
-                    ))
-    return lax.ppermute(x, ("row", "col"), pairs)
+def permute_devices(x, there):
+    count = lax.axis_size("row") * 32
+    return lax.ppermute(x, ("row", "col"), [(i, there(i)) for i in range(count)])
+
+
+def swap(x, axis, bit):
+    step = {"x": 32, "y": 8, "z": 2, "core": 1}[axis] * bit
+    return permute_devices(x, lambda i: i ^ step)
+
+
+def turn_y(x, by):
+    return permute_devices(x, lambda i: i - i % 32 + (i % 32 + 8 * by) % 32)
 
 
 def sum_over_devices(x):
     shape = x.shape
     part = x.reshape(512, 256)
     col = lax.axis_index("col")
-    place = {"core": (col % 2, 2), "y": (col // 8, 4)}
-    for axis in ("core", "y"):
-        me, size = place[axis]
-        rows = part.shape[0] // size
-        total = lax.dynamic_slice_in_dim(part, me * rows, rows)
-        for by in range(1, size):
-            block = lax.dynamic_slice_in_dim(part, (me + by) % size * rows, rows)
-            other = turn_by(block, axis, by)
-            total = total + other
-        part = total
+    core, me = col % 2, col // 8
+    give = jnp.where(core == 1, part[:256], part[256:])
+    other = swap(give, "core", 1)
+    part = jnp.where(core == 1, part[256:], part[:256]) + other
+    total = lax.dynamic_slice_in_dim(part, me * 64, 64)
+    for by in (1, 2, 3):
+        block = lax.dynamic_slice_in_dim(part, (me + by) % 4 * 64, 64)
+        other = turn_y(block, by)
+        total = total + other
+    part = total
     for axis in ("x", "z"):
-        others = [turn_by(part, axis, by) for by in (1, 2, 3)]
-        part = part + others[0] + others[1] + others[2]
-    for axis in ("y", "core"):
-        me, size = place[axis]
-        rows = part.shape[0]
-        joined = jnp.zeros((rows * size, 256), F32)
-        joined = lax.dynamic_update_slice_in_dim(joined, part, me * rows, 0)
-        for by in range(1, size):
-            other = turn_by(part, axis, by)
-            joined = lax.dynamic_update_slice_in_dim(
-                joined, other, (me - by) % size * rows, 0
-            )
-        part = joined
-    return part.reshape(shape)
+        for bit in (1, 2):
+            other = swap(part, axis, bit)
+            part = lax.optimization_barrier(part + other)
+    joined = lax.dynamic_update_slice_in_dim(jnp.zeros((256, 256), F32), part, me * 64, 0)
+    for by in (1, 2, 3):
+        other = turn_y(part, by)
+        joined = lax.dynamic_update_slice_in_dim(joined, other, (me - by) % 4 * 64, 0)
+    other = swap(joined, "core", 1)
+    both = jnp.concatenate([joined, other]), jnp.concatenate([other, joined])
+    return jnp.where(core == 1, both[1], both[0]).reshape(shape)
 
 
 def work(tiles, probe_wave, propagator_phase, positions, slot_count, intensity):
@@ -386,18 +381,19 @@
     strip = tiles[0, :, :WIN]
     lowers = [shift(strip, "row", -1)]
     rest, strip = lax.optimization_barrier((tiles, strip))
-    right = shift(rest[0], "col", -1)
+    first = rest[0]
+    rights = [shift(first, "col", -1)]
+    rest, first = lax.optimization_barrier((rest, first))
     for layer in range(1, layers):
         lowers.append(shift(rest[layer, :, :WIN], "row", -1))
-    tab = jnp.asarray(dft_tables())
+        rights.append(shift(rest[layer], "col", -1))
+    tab = dft_tables()
     phase = parity_order(propagator_phase).reshape(2, 1, HALF, WIN)
     kern = jnp.concatenate([jnp.cos(phase), jnp.sin(phase)], axis=1)
     measured = parity_order(intensity).reshape(slots, 2, HALF, WIN)
-    corner = shift(lowers[0], "col", -1)
-    sides = [(right, corner)]
-    for layer in range(1, layers):
-        joined = jnp.concatenate([rest[layer], lowers[layer]], axis=1)
-        sides.append((shift(joined, "col", -1),))
+    sides = []
+    for layer in range(layers):
+        sides.append((rights[layer], shift(lowers[layer], "col", -1)))
     waves = [probe_wave[None]]
     slabs = []
     for layer in range(last):

time: 306 us -> 261 us (0.85)
  the two profiles are of different devices: /device:TPU:100 before, /device:TPU:1 now
where the time goes in v1:
time: 261 us; the launch traced here: 256 us
  waiting for transfers between devices  90.7 us (35%)
  starting transfers between devices  76.4 us (29%)
  Pallas kernels  44.3 us (17%)
  local copies, waits for them, and re-layouts  26 us (10%)
  other arithmetic  12.3 us (5%)
  matrix products  4.29 us (2%)
    ppermute x21, waiting for transfers between devices, shift(): return lax.ppermute(x, axis, pairs)  57.2 us
    ppermute x21, starting transfers between devices, shift(): return lax.ppermute(x, axis, pairs)  53.9 us
    ppermute x12, waiting for transfers between devices, permute_devices(): lax.ppermute(x, ('row', 'col'), [(i, there(i)) for i in range(count)])  33.5 us
    ppermute x12, starting transfers between devices, permute_devices(): lax.ppermute(x, ('row', 'col'), [(i, there(i)) for i in range(count)])  22.5 us
    pallas_call x3, Pallas kernels, run_forward(): pl.pallas_call(functools.partial(forward_kernel, len(sides)), grid_spec=p...  18.8 us
    pallas_call x3, Pallas kernels, run_backward(): pl.pallas_call(functools.partial(backward_kernel, first), grid_spec=pltpu...  18.7 us
    unnamed x63, local copies, waits for them, and re-layouts  14.5 us
    pallas_call x1, Pallas kernels, run_turn(): pl.pallas_call(functools.partial(turn_kernel, len(sides)), grid_spec=pltp...  6.83 us
  transfers between devices with their start and end apart: 33, of which 14 were waited for; matrix products, arithmetic and copies ran while one was open for 9% of the time, Pallas kernels for 7%

profile of v1, /device:TPU:1, one launch (start us, length us, event | category | flops | bytes accessed | tf_op | source)
XLA Modules:
  0.0 256.3 jit_solution(1432995278118806891)
XLA Ops:
  0.6 1.9 slice_bitcast_fusion.7
  3.9 2.4 slice_bitcast_fusion.3
  6.3 3.3 %collective-permute-start.1 = (f32[2,512,256]{2,1,0:T(8,128)}, f32[2,512,256]{2,1,0:T(8,128)S(1)}, u32[]{:S(2)}, u32[]{:S(2)}) collective-permute-start(f32[2,512,256]{2,1,0:T(8,128)} %slice_bitcast_fusion.3), channel_id=1, source_target_pairs={{1,0},{2,1},{3,2},{4,3},{5,4},{6,5},{7,6},{8,7},{9,8},{10,9},{11,1... | collective-permute-start | bytes 3145736 | tf_op jit(solution)/shard_map/ppermute | solution.py:22
  9.6 2.6 slice_bitcast_fusion.6
  14.9 1.7 slice_bitcast_fusion.2
  16.7 1.9 collective-permute-start.4
  20.2 2.0 copy.9
  22.2 2.1 fusion.15
  25.1 1.9 collective-permute-start.2
  29.1 11.4 %collective-permute-done.3.lower = f32[2,256,256]{2,1,0:T(8,128)} collective-permute-done((f32[2,256,256]{2,1,0:T(8,128)}, f32[2,256,256]{2,1,0:T(8,128)}, u32[]{:S(2)}, u32[]{:S(2)}) %collective-permute-start.3) | collective-permute-done | bytes 524320 | tf_op jit(solution)/shard_map/ppermute | solution.py:22
  42.8 3.6 %collective-permute-start.7 = (f32[2,512,256]{2,1,0:T(8,128)S(1)}, f32[2,512,256]{2,1,0:T(8,128)S(1)}, u32[]{:S(2)}, u32[]{:S(2)}) collective-permute-start(f32[2,512,256]{2,1,0:T(8,128)S(1)} %copy-done.25), channel_id=1, source_target_pairs={{1,0},{2,1},{3,2},{4,3},{5,4},{6,5},{7,6},{8,7},{9,8},{10,9},{11,1... | collective-permute-start | bytes 3145736 | tf_op jit(solution)/shard_map/ppermute | solution.py:22
  46.4 1.9 collective-permute-start.5
  49.6 5.8 %forward.3 = (f32[3,2,256,256]{3,2,1,0:T(8,128)S(1)}, f32[3,2,256,256]{3,2,1,0:T(8,128)S(1)}) custom-call(s32[3,2]{1,0:T(4,128)S(1)} %copy.16.pos, f32[4,2,512,256]{3,2,1,0:T(8,128)S(1)} %copy-done.3, f32[2,256,256]{2,1,0:T(8,128)S(1)} %collective-permute-done.lower, f32[2,512,256]{2,1,0:T(8,128)S(1)} %copy-done.20, ...), custom_call_target="tpu_custom_call" | custom-call | flops 10000000000 | bytes 12582912 | tf_op jit(solution)/shard_map/forward/pallas_call | solution.py:269
  55.4 1.9 collective-permute-start.10
  57.4 1.9 collective-permute-start.11
  59.3 2.1 collective-permute-start.8
  61.4 4.8 %collective-permute-done.5.refs_1_ = f32[2,256,256]{2,1,0:T(8,128)S(1)} collective-permute-done((f32[2,256,256]{2,1,0:T(8,128)}, f32[2,256,256]{2,1,0:T(8,128)S(1)}, u32[]{:S(2)}, u32[]{:S(2)}) %collective-permute-start.5) | collective-permute-done | bytes 524320 | tf_op jit(solution)/shard_map/ppermute | solution.py:22
  66.2 7.2 %forward.4 = (f32[3,2,256,256]{3,2,1,0:T(8,128)S(1)}, f32[3,2,256,256]{3,2,1,0:T(8,128)S(1)}) custom-call(s32[3,2]{1,0:T(4,128)S(1)} %copy.16.pos, f32[4,2,512,256]{3,2,1,0:T(8,128)S(1)} %copy-done.3, f32[2,256,256]{2,1,0:T(8,128)} %collective-permute-done.3.lower, f32[2,512,256]{2,1,0:T(8,128)} %collective-permute-done.4.refs_0_, ...), custom_call_target="tpu_custom_call" | custom-call | flops 10000000000 | bytes 12582912 | tf_op jit(solution)/shard_map/forward/pallas_call | solution.py:269
  73.5 15.2 %collective-permute-done.8.refs_1_ = f32[2,256,256]{2,1,0:T(8,128)S(1)} collective-permute-done((f32[2,256,256]{2,1,0:T(8,128)S(1)}, f32[2,256,256]{2,1,0:T(8,128)S(1)}, u32[]{:S(2)}, u32[]{:S(2)}) %collective-permute-start.8) | collective-permute-done | bytes 524320 | tf_op jit(solution)/shard_map/ppermute | solution.py:22
  88.7 5.8 %forward.5 = (f32[3,2,256,256]{3,2,1,0:T(8,128)S(1)}, f32[3,2,256,256]{3,2,1,0:T(8,128)S(1)}) custom-call(s32[3,2]{1,0:T(4,128)S(1)} %copy.16.pos, f32[4,2,512,256]{3,2,1,0:T(8,128)S(1)} %copy-done.3, f32[2,256,256]{2,1,0:T(8,128)S(1)} %collective-permute-done.6.lower, f32[2,512,256]{2,1,0:T(8,128)S(1)} %collective-permute-done.7.refs_0_, ...), custom_call_target="tpu_custom_call" | custom-call | flops 10000000000 | bytes 12582912 | tf_op jit(solution)/shard_map/forward/pallas_call | solution.py:269
  94.5 6.8 %turn.1 = (f32[2,512,256]{2,1,0:T(8,128)S(1)}, f32[2,256,256]{2,1,0:T(8,128)S(1)}, f32[2,768,256]{2,1,0:T(8,128)S(1)}, f32[3,2,256,256]{3,2,1,0:T(8,128)S(1)}) custom-call(s32[3,2]{1,0:T(4,128)S(1)} %copy.16.pos, s32[1]{0:T(128)S(6)} %copy.25.count, f32[4,2,512,256]{3,2,1,0:T(8,128)S(1)} %copy-done.3, f32[2,256,256]{2,1,0:T(8,128)S(1)} %collective-permute-done.9.lower, ...), custom_call_target="tpu_custom_call" | custom-call | flops 10000000000 | bytes 12582912 | tf_op jit(solution)/shard_map/turn/pallas_call | solution.py:288
  104.3 6.2 %backward.3 = (f32[2,512,256]{2,1,0:T(8,128)S(1)}, f32[2,256,256]{2,1,0:T(8,128)S(1)}, f32[2,768,256]{2,1,0:T(8,128)S(1)}, f32[3,2,256,256]{3,2,1,0:T(8,128)S(1)}) custom-call(s32[3,2]{1,0:T(4,128)S(1)} %copy.16.pos, f32[3,2,256,256]{3,2,1,0:T(8,128)S(1)} %get-tuple-element.81.slab, f32[3,2,256,256]{3,2,1,0:T(8,128)S(1)} %get-tuple-element.80.refs_2_.wave, ...), custom_call_target="tpu_custom_call" | custom-call | flops 10000000000 | bytes 12582912 | tf_op jit(solution)/shard_map/backward/pallas_call | solution.py:308
  111.7 6.2 %backward.4 = (f32[2,512,256]{2,1,0:T(8,128)S(1)}, f32[2,256,256]{2,1,0:T(8,128)S(1)}, f32[2,768,256]{2,1,0:T(8,128)S(1)}, f32[3,2,256,256]{3,2,1,0:T(8,128)S(1)}) custom-call(s32[3,2]{1,0:T(4,128)S(1)} %copy.16.pos, f32[3,2,256,256]{3,2,1,0:T(8,128)S(1)} %get-tuple-element.79.slab, f32[3,2,256,256]{3,2,1,0:T(8,128)S(1)} %get-tuple-element.78.refs_2_.wave, ...), custom_call_target="tpu_custom_call" | custom-call | flops 10000000000 | bytes 12582912 | tf_op jit(solution)/shard_map/backward/pallas_call | solution.py:308
  119.1 6.3 %backward.5 = (f32[2,512,256]{2,1,0:T(8,128)S(1)}, f32[2,256,256]{2,1,0:T(8,128)S(1)}, f32[2,512,256]{2,1,0:T(8,128)S(1)}, f32[2,256,256]{2,1,0:T(8,128)S(1)}, f32[1,2,256,256]{3,2,1,0:T(8,128)S(1)}) custom-call(s32[3,2]{1,0:T(4,128)S(1)} %copy.16.pos, f32[3,2,256,256]{3,2,1,0:T(8,128)S(1)} %get-tuple-element.76.slab, f32[1,2,256,256]{3,2,1,0:T(8,128)S(1)} %bitcast.72, ...), custom_call_target="tpu_custom_call" | custom-call | flops 10000000000 | bytes 12582912 | tf_op jit(solution)/shard_map/backward/pallas_call | solution.py:308
  132.5 3.5 %collective-permute-start.24 = (f32[64,256]{1,0:T(8,128)}, f32[64,256]{1,0:T(8,128)S(1)}, u32[]{:S(2)}, u32[]{:S(2)}) collective-permute-start(f32[64,256]{1,0:T(8,128)} %get-tuple-element.107), channel_id=1, source_target_pairs={{0,24},{1,25},{2,26},{3,27},{4,28},{5,29},{6,30},{7,31},{8,0},{9,1... | collective-permute-start | bytes 196616 | tf_op jit(solution)/shard_map/ppermute | solution.py:338
  136.8 4.0 %collective-permute-start.13 = (f32[2,256,256]{2,1,0:T(8,128)}, f32[2,256,256]{2,1,0:T(8,128)}, u32[]{:S(2)}, u32[]{:S(2)}) collective-permute-start(f32[2,256,256]{2,1,0:T(8,128)} %copy-done.22), channel_id=1, source_target_pairs={{0,1},{1,2},{2,3},{3,4},{4,5},{5,6},{6,7},{7,8},{8,9},{9,10},{10,1... | collective-permute-start | bytes 1572872 | tf_op jit(solution)/shard_map/ppermute | solution.py:22
  140.8 1.9 collective-permute-start.19
  143.6 2.3 collective-permute-start.25
  145.9 1.7 collective-permute-done.25
  147.5 3.1 %collective-permute-start.26 = (f32[64,256]{1,0:T(8,128)S(1)}, f32[64,256]{1,0:T(8,128)S(1)}, u32[]{:S(2)}, u32[]{:S(2)}) collective-permute-start(f32[64,256]{1,0:T(8,128)S(1)} %add.189), channel_id=1, source_target_pairs={{0,64},{1,65},{2,66},{3,67},{4,68},{5,69},{6,70},{7,71},{8,72},{9,... | collective-permute-start | bytes 196616 | tf_op jit(solution)/shard_map/ppermute | solution.py:338
  150.7 5.2 %collective-permute-start.12 = (f32[2,512,256]{2,1,0:T(8,128)}, f32[2,512,256]{2,1,0:T(8,128)}, u32[]{:S(2)}, u32[]{:S(2)}) collective-permute-start(f32[2,512,256]{2,1,0:T(8,128)} %copy-done.18), channel_id=1, source_target_pairs={{0,1},{1,2},{2,3},{3,4},{4,5},{5,6},{6,7},{7,8},{8,9},{9,10},{10,1... | collective-permute-start | bytes 3145736 | tf_op jit(solution)/shard_map/ppermute | solution.py:22
  155.9 2.4 collective-permute-start.27
  158.3 18.9 %collective-permute-done.27 = f32[64,256]{1,0:T(8,128)S(1)} collective-permute-done((f32[64,256]{1,0:T(8,128)S(1)}, f32[64,256]{1,0:T(8,128)S(1)}, u32[]{:S(2)}, u32[]{:S(2)}) %collective-permute-start.27) | collective-permute-done | bytes 65568 | tf_op jit(solution)/shard_map/ppermute | solution.py:338
  177.3 4.0 %collective-permute-start.28 = (f32[64,256]{1,0:T(8,128)S(1)}, f32[64,256]{1,0:T(8,128)S(1)}, u32[]{:S(2)}, u32[]{:S(2)}) collective-permute-start(f32[64,256]{1,0:T(8,128)S(1)} %add.191), channel_id=1, source_target_pairs={{0,4},{1,5},{2,6},{3,7},{4,0},{5,1},{6,2},{7,3},{8,12},{9,13},{10,... | collective-permute-start | bytes 196616 | tf_op jit(solution)/shard_map/ppermute | solution.py:338
  181.3 2.0 collective-permute-start.17
  184.6 4.1 %collective-permute-start.14 = (f32[2,256,256]{2,1,0:T(8,128)S(1)}, f32[2,256,256]{2,1,0:T(8,128)S(1)}, u32[]{:S(2)}, u32[]{:S(2)}) collective-permute-start(f32[2,256,256]{2,1,0:T(8,128)S(1)} %add.163), channel_id=1, source_target_pairs={{0,32},{32,64},{64,96},{1,33},{33,65},{65,97},{2,34},{34,66},{66,9... | collective-permute-start | bytes 1572872 | tf_op jit(solution)/shard_map/ppermute | solution.py:22
  188.8 4.3 %collective-permute-done.29 = f32[64,256]{1,0:T(8,128)S(1)} collective-permute-done((f32[64,256]{1,0:T(8,128)S(1)}, f32[64,256]{1,0:T(8,128)S(1)}, u32[]{:S(2)}, u32[]{:S(2)}) %collective-permute-start.29) | collective-permute-done | bytes 65568 | tf_op jit(solution)/shard_map/ppermute | solution.py:338
  193.5 4.2 %collective-permute-done.30 = f32[64,256]{1,0:T(8,128)S(1)} collective-permute-done((f32[64,256]{1,0:T(8,128)S(1)}, f32[64,256]{1,0:T(8,128)S(1)}, u32[]{:S(2)}, u32[]{:S(2)}) %collective-permute-start.30) | collective-permute-done | bytes 65568 | tf_op jit(solution)/shard_map/ppermute | solution.py:338
  199.2 1.7 collective-permute-done.31
  200.8 4.4 %collective-permute-start.32 = (f32[256,256]{1,0:T(8,128)S(1)}, f32[256,256]{1,0:T(8,128)S(1)}, u32[]{:S(2)}, u32[]{:S(2)}) collective-permute-start(f32[256,256]{1,0:T(8,128)S(1)} %constant_dynamic-update-slice_fusion), channel_id=1, source_target_pairs={{0,1},{1,0},{2,3},{3,2},{4,5},{5,4},{6,7},{7,6},{8,9},{9,8},{10,11... | collective-permute-start | bytes 786440 | tf_op jit(solution)/shard_map/ppermute | solution.py:338
  206.4 3.4 %collective-permute-start.15 = (f32[2,768,256]{2,1,0:T(8,128)S(1)}, f32[2,768,256]{2,1,0:T(8,128)S(1)}, u32[]{:S(2)}, u32[]{:S(2)}) collective-permute-start(f32[2,768,256]{2,1,0:T(8,128)S(1)} %copy-done.15), channel_id=1, source_target_pairs={{0,1},{1,2},{2,3},{3,4},{4,5},{5,6},{6,7},{7,8},{8,9},{9,10},{10,1... | collective-permute-start | bytes 4718600 | tf_op jit(solution)/shard_map/ppermute | solution.py:22
  216.7 3.2 %collective-permute-start.20 = (f32[2,256,256]{2,1,0:T(8,128)S(1)}, f32[2,256,256]{2,1,0:T(8,128)S(1)}, u32[]{:S(2)}, u32[]{:S(2)}) collective-permute-start(f32[2,256,256]{2,1,0:T(8,128)S(1)} %slice_add_fusion.3), channel_id=1, source_target_pairs={{0,32},{32,64},{64,96},{1,33},{33,65},{65,97},{2,34},{34,66},{66,9... | collective-permute-start | bytes 1572872 | tf_op jit(solution)/shard_map/ppermute | solution.py:22
  221.2 3.1 %collective-permute-start.18 = (f32[2,256,256]{2,1,0:T(8,128)S(1)}, f32[2,256,256]{2,1,0:T(8,128)S(1)}, u32[]{:S(2)}, u32[]{:S(2)}) collective-permute-start(f32[2,256,256]{2,1,0:T(8,128)S(1)} %slice_add_fusion.5), channel_id=1, source_target_pairs={{0,32},{32,64},{64,96},{1,33},{33,65},{65,97},{2,34},{34,66},{66,9... | collective-permute-start | bytes 1572872 | tf_op jit(solution)/shard_map/ppermute | solution.py:22
  224.4 2.7 %collective-permute-done.15 = f32[2,768,256]{2,1,0:T(8,128)S(1)} collective-permute-done((f32[2,768,256]{2,1,0:T(8,128)S(1)}, f32[2,768,256]{2,1,0:T(8,128)S(1)}, u32[]{:S(2)}, u32[]{:S(2)}) %collective-permute-start.15) | collective-permute-done | bytes 1572896 | tf_op jit(solution)/shard_map/ppermute | solution.py:22
  227.4 3.2 %collective-permute-start.16 = (f32[2,256,256]{2,1,0:T(8,128)S(1)}, f32[2,256,256]{2,1,0:T(8,128)S(1)}, u32[]{:S(2)}, u32[]{:S(2)}) collective-permute-start(f32[2,256,256]{2,1,0:T(8,128)S(1)} %slice_add_fusion.7), channel_id=1, source_target_pairs={{0,32},{32,64},{64,96},{1,33},{33,65},{65,97},{2,34},{34,66},{66,9... | collective-permute-start | bytes 1572872 | tf_op jit(solution)/shard_map/ppermute | solution.py:22
  231.7 11.2 %collective-permute-done.18 = f32[2,256,256]{2,1,0:T(8,128)S(1)} collective-permute-done((f32[2,256,256]{2,1,0:T(8,128)S(1)}, f32[2,256,256]{2,1,0:T(8,128)S(1)}, u32[]{:S(2)}, u32[]{:S(2)}) %collective-permute-start.18) | collective-permute-done | bytes 524320 | tf_op jit(solution)/shard_map/ppermute | solution.py:22
  243.0 10.8 %collective-permute-done.16 = f32[2,256,256]{2,1,0:T(8,128)S(1)} collective-permute-done((f32[2,256,256]{2,1,0:T(8,128)S(1)}, f32[2,256,256]{2,1,0:T(8,128)S(1)}, u32[]{:S(2)}, u32[]{:S(2)}) %collective-permute-start.16) | collective-permute-done | bytes 524320 | tf_op jit(solution)/shard_map/ppermute | solution.py:22
  253.8 2.5 pad_maximum_fusion
  (129 shorter events, 39.1 us)
Async XLA Ops:
  0.6 23.7 %copy-start = (f32[3,256,256]{2,1,0:T(8,128)S(1)}, f32[3,256,256]{2,1,0:T(8,128)}, u32[]{:S(2)}) copy-start(f32[3,256,256]{2,1,0:T(8,128)} %param.20) | copy-start | bytes 2359300
  2.6 22.5 %collective-permute-start = (f32[2,256,256]{2,1,0:T(8,128)}, f32[2,256,256]{2,1,0:T(8,128)S(1)}, u32[]{:S(2)}, u32[]{:S(2)}) collective-permute-start(f32[2,256,256]{2,1,0:T(8,128)} %slice_bitcast_fusion.7), channel_id=1, source_target_pairs={{32,0},{64,32},{96,64},{33,1},{65,33},{97,65},{34,2},{66,34},{98,6... | collective-permute-start | bytes 1572872 | tf_op jit(solution)/shard_map/ppermute | solution.py:22
  3.9 11.1 %copy-start.2 = (f32[4,2,512,256]{3,2,1,0:T(8,128)S(1)}, f32[4,2,512,256]{3,2,1,0:T(8,128)}, u32[]{:S(2)}) copy-start(f32[4,2,512,256]{3,2,1,0:T(8,128)} %own.7) | copy-start | bytes 12582916
  6.3 35.5 %collective-permute-start.1 = (f32[2,512,256]{2,1,0:T(8,128)}, f32[2,512,256]{2,1,0:T(8,128)S(1)}, u32[]{:S(2)}, u32[]{:S(2)}) collective-permute-start(f32[2,512,256]{2,1,0:T(8,128)} %slice_bitcast_fusion.3), channel_id=1, source_target_pairs={{1,0},{2,1},{3,2},{4,3},{5,4},{6,5},{7,6},{8,7},{9,8},{10,9},{11,1... | collective-permute-start | bytes 3145736 | tf_op jit(solution)/shard_map/ppermute | solution.py:22
  12.2 43.2 %collective-permute-start.9 = (f32[2,256,256]{2,1,0:T(8,128)}, f32[2,256,256]{2,1,0:T(8,128)S(1)}, u32[]{:S(2)}, u32[]{:S(2)}) collective-permute-start(f32[2,256,256]{2,1,0:T(8,128)} %get-tuple-element.104), channel_id=1, source_target_pairs={{32,0},{64,32},{96,64},{33,1},{65,33},{97,65},{34,2},{66,34},{98,6... | collective-permute-start | bytes 1572872 | tf_op jit(solution)/shard_map/ppermute | solution.py:22
  13.5 5.2 %copy-start.28 = (f32[256,256]{1,0:T(8,128)S(1)}, f32[256,256]{1,0:T(8,128)}, u32[]{:S(2)}) copy-start(f32[256,256]{1,0:T(8,128)} %param.17) | copy-start | bytes 786436
  13.5 5.9 %copy-start.27 = (s32[3,2]{0,1:T(2,128)S(1)}, s32[3,2]{0,1:T(2,128)}, u32[]{:S(2)}) copy-start(s32[3,2]{0,1:T(2,128)} %param.18) | copy-start | bytes 76
  13.5 27.0 %collective-permute-start.3 = (f32[2,256,256]{2,1,0:T(8,128)}, f32[2,256,256]{2,1,0:T(8,128)}, u32[]{:S(2)}, u32[]{:S(2)}) collective-permute-start(f32[2,256,256]{2,1,0:T(8,128)} %get-tuple-element.103), channel_id=1, source_target_pairs={{32,0},{64,32},{96,64},{33,1},{65,33},{97,65},{34,2},{66,34},{98,6... | collective-permute-start | bytes 1572872 | tf_op jit(solution)/shard_map/ppermute | solution.py:22
  16.7 42.6 %collective-permute-start.4 = (f32[2,512,256]{2,1,0:T(8,128)}, f32[2,512,256]{2,1,0:T(8,128)}, u32[]{:S(2)}, u32[]{:S(2)}) collective-permute-start(f32[2,512,256]{2,1,0:T(8,128)} %get-tuple-element.100), channel_id=1, source_target_pairs={{1,0},{2,1},{3,2},{4,3},{5,4},{6,5},{7,6},{8,7},{9,8},{10,9},{11,1... | collective-permute-start | bytes 3145736 | tf_op jit(solution)/shard_map/ppermute | solution.py:22
  22.2 4.8 %copy-start.23 = (bf16[2,1,2,256,256]{4,3,2,1,0:T(8,128)(2,1)S(1)}, bf16[2,1,2,256,256]{4,3,2,1,0:T(8,128)(2,1)}, u32[]{:S(2)}) copy-start(bf16[2,1,2,256,256]{4,3,2,1,0:T(8,128)(2,1)} %copy.9) | copy-start | bytes 1572868
  24.3 16.2 %copy-start.26 = (f32[2,256,256]{2,1,0:T(8,128)S(1)}, f32[2,256,256]{2,1,0:T(8,128)}, u32[]{:S(2)}) copy-start(f32[2,256,256]{2,1,0:T(8,128)} %get-tuple-element.105) | copy-start | bytes 1572868
  24.3 18.5 %copy-start.25 = (f32[2,512,256]{2,1,0:T(8,128)S(1)}, f32[2,512,256]{2,1,0:T(8,128)}, u32[]{:S(2)}) copy-start(f32[2,512,256]{2,1,0:T(8,128)} %get-tuple-element.102) | copy-start | bytes 3145732
  25.1 21.3 %collective-permute-start.2 = (f32[2,256,256]{2,1,0:T(8,128)S(1)}, f32[2,256,256]{2,1,0:T(8,128)S(1)}, u32[]{:S(2)}, u32[]{:S(2)}) collective-permute-start(f32[2,256,256]{2,1,0:T(8,128)S(1)} %collective-permute-done.lower), channel_id=1, source_target_pairs={{1,0},{2,1},{3,2},{4,3},{5,4},{6,5},{7,6},{8,7},{9,8},{10,9},{11,1... | collective-permute-start | bytes 1572872 | tf_op jit(solution)/shard_map/ppermute | solution.py:22
  27.0 21.3 %copy-start.3 = (f32[4,2,512,256]{3,2,1,0:T(8,128)S(1)}, f32[4,2,512,256]{3,2,1,0:T(8,128)}, u32[]{:S(2)}) copy-start(f32[4,2,512,256]{3,2,1,0:T(8,128)} %own.7) | copy-start | bytes 12582916
  28.3 20.0 %copy-start.21 = (f32[2,256,256]{2,1,0:T(8,128)S(1)}, f32[2,256,256]{2,1,0:T(8,128)}, u32[]{:S(2)}) copy-start(f32[2,256,256]{2,1,0:T(8,128)} %param.16) | copy-start | bytes 1572868
  40.5 16.8 %collective-permute-start.6 = (f32[2,256,256]{2,1,0:T(8,128)S(1)}, f32[2,256,256]{2,1,0:T(8,128)S(1)}, u32[]{:S(2)}, u32[]{:S(2)}) collective-permute-start(f32[2,256,256]{2,1,0:T(8,128)S(1)} %copy-done.26), channel_id=1, source_target_pairs={{32,0},{64,32},{96,64},{33,1},{65,33},{97,65},{34,2},{66,34},{98,6... | collective-permute-start | bytes 1572872 | tf_op jit(solution)/shard_map/ppermute | solution.py:22
  42.8 30.6 %collective-permute-start.7 = (f32[2,512,256]{2,1,0:T(8,128)S(1)}, f32[2,512,256]{2,1,0:T(8,128)S(1)}, u32[]{:S(2)}, u32[]{:S(2)}) collective-permute-start(f32[2,512,256]{2,1,0:T(8,128)S(1)} %copy-done.25), channel_id=1, source_target_pairs={{1,0},{2,1},{3,2},{4,3},{5,4},{6,5},{7,6},{8,7},{9,8},{10,9},{11,1... | collective-permute-start | bytes 3145736 | tf_op jit(solution)/shard_map/ppermute | solution.py:22
  46.4 19.8 %collective-permute-start.5 = (f32[2,256,256]{2,1,0:T(8,128)}, f32[2,256,256]{2,1,0:T(8,128)S(1)}, u32[]{:S(2)}, u32[]{:S(2)}) collective-permute-start(f32[2,256,256]{2,1,0:T(8,128)} %collective-permute-done.3.lower), channel_id=1, source_target_pairs={{1,0},{2,1},{3,2},{4,3},{5,4},{6,5},{7,6},{8,7},{9,8},{10,9},{11,1... | collective-permute-start | bytes 1572872 | tf_op jit(solution)/shard_map/ppermute | solution.py:22
  49.6 5.8 %copy-start.24 = (f32[2,512,256]{2,1,0:T(8,128)S(1)}, f32[2,512,256]{2,1,0:T(8,128)}, u32[]{:S(2)}) copy-start(f32[2,512,256]{2,1,0:T(8,128)} %get-tuple-element.101) | copy-start | bytes 3145732
  55.4 39.1 %collective-permute-start.10 = (f32[2,512,256]{2,1,0:T(8,128)S(1)}, f32[2,512,256]{2,1,0:T(8,128)S(1)}, u32[]{:S(2)}, u32[]{:S(2)}) collective-permute-start(f32[2,512,256]{2,1,0:T(8,128)S(1)} %copy-done.24), channel_id=1, source_target_pairs={{1,0},{2,1},{3,2},{4,3},{5,4},{6,5},{7,6},{8,7},{9,8},{10,9},{11,1... | collective-permute-start | bytes 3145736 | tf_op jit(solution)/shard_map/ppermute | solution.py:22
  57.4 37.2 %collective-permute-start.11 = (f32[2,256,256]{2,1,0:T(8,128)S(1)}, f32[2,256,256]{2,1,0:T(8,128)S(1)}, u32[]{:S(2)}, u32[]{:S(2)}) collective-permute-start(f32[2,256,256]{2,1,0:T(8,128)S(1)} %collective-permute-done.9.lower), channel_id=1, source_target_pairs={{1,0},{2,1},{3,2},{4,3},{5,4},{6,5},{7,6},{8,7},{9,8},{10,9},{11,1... | collective-permute-start | bytes 1572872 | tf_op jit(solution)/shard_map/ppermute | solution.py:22
  59.3 29.4 %collective-permute-start.8 = (f32[2,256,256]{2,1,0:T(8,128)S(1)}, f32[2,256,256]{2,1,0:T(8,128)S(1)}, u32[]{:S(2)}, u32[]{:S(2)}) collective-permute-start(f32[2,256,256]{2,1,0:T(8,128)S(1)} %collective-permute-done.6.lower), channel_id=1, source_target_pairs={{1,0},{2,1},{3,2},{4,3},{5,4},{6,5},{7,6},{8,7},{9,8},{10,9},{11,1... | collective-permute-start | bytes 1572872 | tf_op jit(solution)/shard_map/ppermute | solution.py:22
  111.7 6.2 %copy-start.8 = (f32[2,256,256]{2,1,0:T(8,128)}, f32[2,256,256]{2,1,0:T(8,128)S(1)}, u32[]{:S(2)}) copy-start(f32[2,256,256]{2,1,0:T(8,128)S(1)} %get-tuple-element.95) | copy-start | bytes 1572868
  129.0 1.7 collective-permute-start.21
  131.8 51.6 %copy-start.13 = (f32[2,256,256]{2,1,0:T(8,128)S(1)}, f32[2,256,256]{2,1,0:T(8,128)}, u32[]{:S(2)}) copy-start(f32[2,256,256]{2,1,0:T(8,128)} %copy-done.12) | copy-start | bytes 1572868
  132.5 10.2 %collective-permute-start.24 = (f32[64,256]{1,0:T(8,128)}, f32[64,256]{1,0:T(8,128)S(1)}, u32[]{:S(2)}, u32[]{:S(2)}) collective-permute-start(f32[64,256]{1,0:T(8,128)} %get-tuple-element.107), channel_id=1, source_target_pairs={{0,24},{1,25},{2,26},{3,27},{4,28},{5,29},{6,30},{7,31},{8,0},{9,1... | collective-permute-start | bytes 196616 | tf_op jit(solution)/shard_map/ppermute | solution.py:338
  136.0 6.7 %collective-permute-start.23 = (f32[64,256]{1,0:T(8,128)}, f32[64,256]{1,0:T(8,128)S(1)}, u32[]{:S(2)}, u32[]{:S(2)}) collective-permute-start(f32[64,256]{1,0:T(8,128)} %get-tuple-element.108), channel_id=1, source_target_pairs={{0,16},{1,17},{2,18},{3,19},{4,20},{5,21},{6,22},{7,23},{8,24},{9,... | collective-permute-start | bytes 196616 | tf_op jit(solution)/shard_map/ppermute | solution.py:338
  136.1 6.7 %collective-permute-start.22 = (f32[64,256]{1,0:T(8,128)}, f32[64,256]{1,0:T(8,128)}, u32[]{:S(2)}, u32[]{:S(2)}) collective-permute-start(f32[64,256]{1,0:T(8,128)} %get-tuple-element.106), channel_id=1, source_target_pairs={{0,8},{1,9},{2,10},{3,11},{4,12},{5,13},{6,14},{7,15},{8,16},{9,17... | collective-permute-start | bytes 196616 | tf_op jit(solution)/shard_map/ppermute | solution.py:338
  136.8 46.6 %collective-permute-start.13 = (f32[2,256,256]{2,1,0:T(8,128)}, f32[2,256,256]{2,1,0:T(8,128)}, u32[]{:S(2)}, u32[]{:S(2)}) collective-permute-start(f32[2,256,256]{2,1,0:T(8,128)} %copy-done.22), channel_id=1, source_target_pairs={{0,1},{1,2},{2,3},{3,4},{4,5},{5,6},{6,7},{7,8},{8,9},{9,10},{10,1... | collective-permute-start | bytes 1572872 | tf_op jit(solution)/shard_map/ppermute | solution.py:22
  140.8 71.4 %collective-permute-start.19 = (f32[2,768,256]{2,1,0:T(8,128)}, f32[2,768,256]{2,1,0:T(8,128)}, u32[]{:S(2)}, u32[]{:S(2)}) collective-permute-start(f32[2,768,256]{2,1,0:T(8,128)} %copy-done.17), channel_id=1, source_target_pairs={{0,1},{1,2},{2,3},{3,4},{4,5},{5,6},{6,7},{7,8},{8,9},{9,10},{10,1... | collective-permute-start | bytes 4718600 | tf_op jit(solution)/shard_map/ppermute | solution.py:22
  143.6 3.9 %collective-permute-start.25 = (f32[64,256]{1,0:T(8,128)S(1)}, f32[64,256]{1,0:T(8,128)S(1)}, u32[]{:S(2)}, u32[]{:S(2)}) collective-permute-start(f32[64,256]{1,0:T(8,128)S(1)} %add_add_fusion), channel_id=1, source_target_pairs={{0,32},{1,33},{2,34},{3,35},{4,36},{5,37},{6,38},{7,39},{8,40},{9,... | collective-permute-start | bytes 196616 | tf_op jit(solution)/shard_map/ppermute | solution.py:338
  147.5 8.3 %collective-permute-start.26 = (f32[64,256]{1,0:T(8,128)S(1)}, f32[64,256]{1,0:T(8,128)S(1)}, u32[]{:S(2)}, u32[]{:S(2)}) collective-permute-start(f32[64,256]{1,0:T(8,128)S(1)} %add.189), channel_id=1, source_target_pairs={{0,64},{1,65},{2,66},{3,67},{4,68},{5,69},{6,70},{7,71},{8,72},{9,... | collective-permute-start | bytes 196616 | tf_op jit(solution)/shard_map/ppermute | solution.py:338
  150.7 59.9 %collective-permute-start.12 = (f32[2,512,256]{2,1,0:T(8,128)}, f32[2,512,256]{2,1,0:T(8,128)}, u32[]{:S(2)}, u32[]{:S(2)}) collective-permute-start(f32[2,512,256]{2,1,0:T(8,128)} %copy-done.18), channel_id=1, source_target_pairs={{0,1},{1,2},{2,3},{3,4},{4,5},{5,6},{6,7},{7,8},{8,9},{9,10},{10,1... | collective-permute-start | bytes 3145736 | tf_op jit(solution)/shard_map/ppermute | solution.py:22
  155.9 21.4 %collective-permute-start.27 = (f32[64,256]{1,0:T(8,128)S(1)}, f32[64,256]{1,0:T(8,128)S(1)}, u32[]{:S(2)}, u32[]{:S(2)}) collective-permute-start(f32[64,256]{1,0:T(8,128)S(1)} %add.190), channel_id=1, source_target_pairs={{0,2},{1,3},{2,0},{3,1},{4,6},{5,7},{6,4},{7,5},{8,10},{9,11},{10,... | collective-permute-start | bytes 196616 | tf_op jit(solution)/shard_map/ppermute | solution.py:338
  177.3 11.4 %collective-permute-start.28 = (f32[64,256]{1,0:T(8,128)S(1)}, f32[64,256]{1,0:T(8,128)S(1)}, u32[]{:S(2)}, u32[]{:S(2)}) collective-permute-start(f32[64,256]{1,0:T(8,128)S(1)} %add.191), channel_id=1, source_target_pairs={{0,4},{1,5},{2,6},{3,7},{4,0},{5,1},{6,2},{7,3},{8,12},{9,13},{10,... | collective-permute-start | bytes 196616 | tf_op jit(solution)/shard_map/ppermute | solution.py:338
  181.3 25.1 %copy-start.15 = (f32[2,768,256]{2,1,0:T(8,128)S(1)}, f32[2,768,256]{2,1,0:T(8,128)}, u32[]{:S(2)}) copy-start(f32[2,768,256]{2,1,0:T(8,128)} %copy-done.14) | copy-start | bytes 4718596
  181.3 38.6 %collective-permute-start.17 = (f32[2,768,256]{2,1,0:T(8,128)}, f32[2,768,256]{2,1,0:T(8,128)S(1)}, u32[]{:S(2)}, u32[]{:S(2)}) collective-permute-start(f32[2,768,256]{2,1,0:T(8,128)} %copy-done.16), channel_id=1, source_target_pairs={{0,1},{1,2},{2,3},{3,4},{4,5},{5,6},{6,7},{7,8},{8,9},{9,10},{10,1... | collective-permute-start | bytes 4718600 | tf_op jit(solution)/shard_map/ppermute | solution.py:22
  183.4 27.2 %copy-start.7 = (f32[2,512,256]{2,1,0:T(8,128)S(1)}, f32[2,512,256]{2,1,0:T(8,128)}, u32[]{:S(2)}) copy-start(f32[2,512,256]{2,1,0:T(8,128)} %copy-done.6) | copy-start | bytes 3145732
  184.6 27.5 %collective-permute-start.14 = (f32[2,256,256]{2,1,0:T(8,128)S(1)}, f32[2,256,256]{2,1,0:T(8,128)S(1)}, u32[]{:S(2)}, u32[]{:S(2)}) collective-permute-start(f32[2,256,256]{2,1,0:T(8,128)S(1)} %add.163), channel_id=1, source_target_pairs={{0,32},{32,64},{64,96},{1,33},{33,65},{65,97},{2,34},{34,66},{66,9... | collective-permute-start | bytes 1572872 | tf_op jit(solution)/shard_map/ppermute | solution.py:22
  188.7 4.4 %collective-permute-start.29 = (f32[64,256]{1,0:T(8,128)S(1)}, f32[64,256]{1,0:T(8,128)S(1)}, u32[]{:S(2)}, u32[]{:S(2)}) collective-permute-start(f32[64,256]{1,0:T(8,128)S(1)} %add.192), channel_id=1, source_target_pairs={{0,8},{1,9},{2,10},{3,11},{4,12},{5,13},{6,14},{7,15},{8,16},{9,17... | collective-permute-start | bytes 196616 | tf_op jit(solution)/shard_map/ppermute | solution.py:338
  193.1 4.6 %collective-permute-start.30 = (f32[64,256]{1,0:T(8,128)S(1)}, f32[64,256]{1,0:T(8,128)S(1)}, u32[]{:S(2)}, u32[]{:S(2)}) collective-permute-start(f32[64,256]{1,0:T(8,128)S(1)} %add.192), channel_id=1, source_target_pairs={{0,16},{1,17},{2,18},{3,19},{4,20},{5,21},{6,22},{7,23},{8,24},{9,... | collective-permute-start | bytes 196616 | tf_op jit(solution)/shard_map/ppermute | solution.py:338
  197.7 3.1 %collective-permute-start.31 = (f32[64,256]{1,0:T(8,128)S(1)}, f32[64,256]{1,0:T(8,128)S(1)}, u32[]{:S(2)}, u32[]{:S(2)}) collective-permute-start(f32[64,256]{1,0:T(8,128)S(1)} %add.192), channel_id=1, source_target_pairs={{0,24},{1,25},{2,26},{3,27},{4,28},{5,29},{6,30},{7,31},{8,0},{9,1... | collective-permute-start | bytes 196616 | tf_op jit(solution)/shard_map/ppermute | solution.py:338
  200.8 5.6 %collective-permute-start.32 = (f32[256,256]{1,0:T(8,128)S(1)}, f32[256,256]{1,0:T(8,128)S(1)}, u32[]{:S(2)}, u32[]{:S(2)}) collective-permute-start(f32[256,256]{1,0:T(8,128)S(1)} %constant_dynamic-update-slice_fusion), channel_id=1, source_target_pairs={{0,1},{1,0},{2,3},{3,2},{4,5},{5,4},{6,7},{7,6},{8,9},{9,8},{10,11... | collective-permute-start | bytes 786440 | tf_op jit(solution)/shard_map/ppermute | solution.py:338
  206.4 20.7 %collective-permute-start.15 = (f32[2,768,256]{2,1,0:T(8,128)S(1)}, f32[2,768,256]{2,1,0:T(8,128)S(1)}, u32[]{:S(2)}, u32[]{:S(2)}) collective-permute-start(f32[2,768,256]{2,1,0:T(8,128)S(1)} %copy-done.15), channel_id=1, source_target_pairs={{0,1},{1,2},{2,3},{3,4},{4,5},{5,6},{6,7},{7,8},{8,9},{9,10},{10,1... | collective-permute-start | bytes 4718600 | tf_op jit(solution)/shard_map/ppermute | solution.py:22
  216.7 14.9 %collective-permute-start.20 = (f32[2,256,256]{2,1,0:T(8,128)S(1)}, f32[2,256,256]{2,1,0:T(8,128)S(1)}, u32[]{:S(2)}, u32[]{:S(2)}) collective-permute-start(f32[2,256,256]{2,1,0:T(8,128)S(1)} %slice_add_fusion.3), channel_id=1, source_target_pairs={{0,32},{32,64},{64,96},{1,33},{33,65},{65,97},{2,34},{34,66},{66,9... | collective-permute-start | bytes 1572872 | tf_op jit(solution)/shard_map/ppermute | solution.py:22
  221.2 21.7 %collective-permute-start.18 = (f32[2,256,256]{2,1,0:T(8,128)S(1)}, f32[2,256,256]{2,1,0:T(8,128)S(1)}, u32[]{:S(2)}, u32[]{:S(2)}) collective-permute-start(f32[2,256,256]{2,1,0:T(8,128)S(1)} %slice_add_fusion.5), channel_id=1, source_target_pairs={{0,32},{32,64},{64,96},{1,33},{33,65},{65,97},{2,34},{34,66},{66,9... | collective-permute-start | bytes 1572872 | tf_op jit(solution)/shard_map/ppermute | solution.py:22
  227.4 26.3 %collective-permute-start.16 = (f32[2,256,256]{2,1,0:T(8,128)S(1)}, f32[2,256,256]{2,1,0:T(8,128)S(1)}, u32[]{:S(2)}, u32[]{:S(2)}) collective-permute-start(f32[2,256,256]{2,1,0:T(8,128)S(1)} %slice_add_fusion.7), channel_id=1, source_target_pairs={{0,32},{32,64},{64,96},{1,33},{33,65},{65,97},{2,34},{34,66},{66,9... | collective-permute-start | bytes 1572872 | tf_op jit(solution)/shard_map/ppermute | solution.py:22
  253.8 2.5 copy-start.1
  (14 other events, 14.4 us)

commit v2 on v1

--- a/solution.py
+++ b/solution.py
@@ -374,26 +374,39 @@
     return jnp.where(core == 1, both[1], both[0]).reshape(shape)
 
 
+def corner_by_row(right, lower):
+    rows, cols = lax.axis_size("row"), lax.axis_size("col")
+    up = [((r + 1) * cols + c, r * cols + c) for r in range(rows - 1) for c in range(1, cols, 2)]
+    near = [(r * cols + c + 1, r * cols + c) for r in range(rows) for c in range(0, cols, 2)]
+    from_below = lax.ppermute(right[:, :WIN], ("row", "col"), up)
+    from_core = lax.ppermute(lower, ("row", "col"), near)
+    return jnp.where(lax.axis_index("col") % 2 == 1, from_below, from_core)
+
+
 def work(tiles, probe_wave, propagator_phase, positions, slot_count, intensity):
     layers = tiles.shape[0]
     slots = positions.shape[0]
     last = layers - 1
-    strip = tiles[0, :, :WIN]
+    first = tiles[0]
+    rights = [shift(first, "col", -1)]
+    rest, first = lax.optimization_barrier((tiles, first))
+    strip = rest[0, :, :WIN]
     lowers = [shift(strip, "row", -1)]
-    rest, strip = lax.optimization_barrier((tiles, strip))
-    first = rest[0]
-    rights = [shift(first, "col", -1)]
-    rest, first = lax.optimization_barrier((rest, first))
+    rest, strip = lax.optimization_barrier((rest, strip))
     for layer in range(1, layers):
+        rights.append(shift(rest[layer], "col", -1))
         lowers.append(shift(rest[layer, :, :WIN], "row", -1))
-        rights.append(shift(rest[layer], "col", -1))
     tab = dft_tables()
     phase = parity_order(propagator_phase).reshape(2, 1, HALF, WIN)
     kern = jnp.concatenate([jnp.cos(phase), jnp.sin(phase)], axis=1)
     measured = parity_order(intensity).reshape(slots, 2, HALF, WIN)
     sides = []
     for layer in range(layers):
-        sides.append((rights[layer], shift(lowers[layer], "col", -1)))
+        if layer == 1:
+            corner = corner_by_row(rights[layer], lowers[layer])
+        else:
+            corner = shift(lowers[layer], "col", -1)
+        sides.append((rights[layer], corner))
     waves = [probe_wave[None]]
     slabs = []
     for layer in range(last):

time: 261 us -> 262 us (level)
  starting transfers between devices: 76.4 us -> 83.8 us
  waiting for transfers between devices: 90.7 us -> 84.8 us
    ppermute x12, starting transfers between devices: 22.5 us -> 27.8 us  [permute_devices(): lax.ppermute(x, ('row', 'col'), [(i, there(i)) for i in range(count)])]
    ppermute x21 -> x20, waiting for transfers between devices: 57.2 us -> 53.3 us  [shift(): return lax.ppermute(x, axis, pairs)]
    ppermute x0 -> x2, starting transfers between devices: none -> 3.62 us  [the longest x1 2.33 us: corner_by_row(): from_core = lax.ppermute(lower, ('row', 'col'), near)]
    unnamed x63 -> x59, local copies, waits for them, and re-layouts: 14.5 us -> 12.4 us
    ppermute x21 -> x20, starting transfers between devices: 53.9 us -> 52.4 us  [shift(): return lax.ppermute(x, axis, pairs)]
  transfers between devices with their start and end apart: 33 -> 34, of which waited for: 14 -> 18; matrix products, arithmetic and copies ran while one was open for 9% -> 9% of each run, Pallas kernels for 7% -> 8%
where the time goes in v2:
time: 262 us; the launch traced here: 257 us
  waiting for transfers between devices  84.8 us (32%)
  starting transfers between devices  83.8 us (32%)
  Pallas kernels  45.2 us (17%)
  local copies, waits for them, and re-layouts  23.9 us (9%)
  other arithmetic  12.4 us (5%)
  matrix products  4.29 us (2%)
    ppermute x20, waiting for transfers between devices, shift(): return lax.ppermute(x, axis, pairs)  53.3 us
    ppermute x20, starting transfers between devices, shift(): return lax.ppermute(x, axis, pairs)  52.4 us
    ppermute x12, waiting for transfers between devices, permute_devices(): lax.ppermute(x, ('row', 'col'), [(i, there(i)) for i in range(count)])  31.4 us
    ppermute x12, starting transfers between devices, permute_devices(): lax.ppermute(x, ('row', 'col'), [(i, there(i)) for i in range(count)])  27.8 us
    pallas_call x3, Pallas kernels, run_forward(): pl.pallas_call(functools.partial(forward_kernel, len(sides)), grid_spec=p...  19.7 us
    pallas_call x3, Pallas kernels, run_backward(): pl.pallas_call(functools.partial(backward_kernel, first), grid_spec=pltpu...  18.7 us
    unnamed x59, local copies, waits for them, and re-layouts  12.4 us
    pallas_call x1, Pallas kernels, run_turn(): pl.pallas_call(functools.partial(turn_kernel, len(sides)), grid_spec=pltp...  6.83 us
  transfers between devices with their start and end apart: 34, of which 18 were waited for; matrix products, arithmetic and copies ran while one was open for 9% of the time, Pallas kernels for 8%

profile of v2, /device:TPU:1, one launch (start us, length us, event | category | flops | bytes accessed | tf_op | source)
XLA Modules:
  0.0 256.6 jit_solution(9011391154430411856)
XLA Ops:
  0.6 2.4 slice_bitcast_fusion.3
  3.0 3.3 %collective-permute-start.1 = (f32[2,512,256]{2,1,0:T(8,128)}, f32[2,512,256]{2,1,0:T(8,128)}, u32[]{:S(2)}, u32[]{:S(2)}) collective-permute-start(f32[2,512,256]{2,1,0:T(8,128)} %slice_bitcast_fusion.3), channel_id=1, source_target_pairs={{1,0},{2,1},{3,2},{4,3},{5,4},{6,5},{7,6},{8,7},{9,8},{10,9},{11,1... | collective-permute-start | bytes 3145736 | tf_op jit(solution)/shard_map/ppermute | solution.py:22
  6.3 2.0 slice_bitcast_fusion.7
  9.6 2.6 slice_bitcast_fusion.6
  15.0 1.7 slice_bitcast_fusion.2
  16.7 1.9 collective-permute-start.4
  20.2 2.0 copy.9
  22.3 2.1 fusion.15
  25.8 1.9 collective-permute-start.2
  29.2 4.2 %collective-permute-done.4.refs_0_ = f32[2,512,256]{2,1,0:T(8,128)S(1)} collective-permute-done((f32[2,512,256]{2,1,0:T(8,128)}, f32[2,512,256]{2,1,0:T(8,128)S(1)}, u32[]{:S(2)}, u32[]{:S(2)}) %collective-permute-start.4) | collective-permute-done | bytes 1048608 | tf_op jit(solution)/shard_map/ppermute | solution.py:22
  33.3 1.9 collective-permute-start.11
  35.3 11.4 %collective-permute-done.3.lower = f32[2,256,256]{2,1,0:T(8,128)} collective-permute-done((f32[2,256,256]{2,1,0:T(8,128)}, f32[2,256,256]{2,1,0:T(8,128)}, u32[]{:S(2)}, u32[]{:S(2)}) %collective-permute-start.3) | collective-permute-done | bytes 524320 | tf_op jit(solution)/shard_map/ppermute | solution.py:22
  48.0 2.3 collective-permute-start.6
  51.6 7.0 %forward.3 = (f32[3,2,256,256]{3,2,1,0:T(8,128)S(1)}, f32[3,2,256,256]{3,2,1,0:T(8,128)S(1)}) custom-call(s32[3,2]{1,0:T(4,128)S(1)} %copy.16.pos, f32[4,2,512,256]{3,2,1,0:T(8,128)S(1)} %copy-done.3, f32[2,256,256]{2,1,0:T(8,128)S(1)} %collective-permute-done.lower, f32[2,512,256]{2,1,0:T(8,128)} %collective-permute-done.1.refs_0_, ...), custom_call_target="tpu_custom_call" | custom-call | flops 10000000000 | bytes 12582912 | tf_op jit(solution)/shard_map/forward/pallas_call | solution.py:269
  58.7 1.9 collective-permute-start.8
  61.6 4.0 %collective-permute-start.12 = (f32[2,256,256]{2,1,0:T(8,128)S(1)}, f32[2,256,256]{2,1,0:T(8,128)S(1)}, u32[]{:S(2)}, u32[]{:S(2)}) collective-permute-start(f32[2,256,256]{2,1,0:T(8,128)S(1)} %collective-permute-done.10.lower), channel_id=1, source_target_pairs={{1,0},{2,1},{3,2},{4,3},{5,4},{6,5},{7,6},{8,7},{9,8},{10,9},{11,1... | collective-permute-start | bytes 1572872 | tf_op jit(solution)/shard_map/ppermute | solution.py:22
  65.6 2.1 collective-permute-start.9
  67.9 6.9 %forward.4 = (f32[3,2,256,256]{3,2,1,0:T(8,128)S(1)}, f32[3,2,256,256]{3,2,1,0:T(8,128)S(1)}) custom-call(s32[3,2]{1,0:T(4,128)S(1)} %copy.16.pos, f32[4,2,512,256]{3,2,1,0:T(8,128)S(1)} %copy-done.3, f32[2,256,256]{2,1,0:T(8,128)} %collective-permute-done.3.lower, f32[2,512,256]{2,1,0:T(8,128)S(1)} %collective-permute-done.4.refs_0_, ...), custom_call_target="tpu_custom_call" | custom-call | flops 10000000000 | bytes 12582912 | tf_op jit(solution)/shard_map/forward/pallas_call | solution.py:269
  74.8 11.2 %collective-permute-done.9.refs_1_ = f32[2,256,256]{2,1,0:T(8,128)S(1)} collective-permute-done((f32[2,256,256]{2,1,0:T(8,128)S(1)}, f32[2,256,256]{2,1,0:T(8,128)S(1)}, u32[]{:S(2)}, u32[]{:S(2)}) %collective-permute-start.9) | collective-permute-done | bytes 524320 | tf_op jit(solution)/shard_map/ppermute | solution.py:22
  86.0 5.8 %forward.5 = (f32[3,2,256,256]{3,2,1,0:T(8,128)S(1)}, f32[3,2,256,256]{3,2,1,0:T(8,128)S(1)}) custom-call(s32[3,2]{1,0:T(4,128)S(1)} %copy.16.pos, f32[4,2,512,256]{3,2,1,0:T(8,128)S(1)} %copy-done.3, f32[2,256,256]{2,1,0:T(8,128)S(1)} %collective-permute-done.7.lower, f32[2,512,256]{2,1,0:T(8,128)S(1)} %collective-permute-done.8.refs_0_, ...), custom_call_target="tpu_custom_call" | custom-call | flops 10000000000 | bytes 12582912 | tf_op jit(solution)/shard_map/forward/pallas_call | solution.py:269
  91.9 6.8 %turn.1 = (f32[2,512,256]{2,1,0:T(8,128)S(1)}, f32[2,256,256]{2,1,0:T(8,128)S(1)}, f32[2,768,256]{2,1,0:T(8,128)S(1)}, f32[3,2,256,256]{3,2,1,0:T(8,128)S(1)}) custom-call(s32[3,2]{1,0:T(4,128)S(1)} %copy.16.pos, s32[1]{0:T(128)S(6)} %copy.25.count, f32[4,2,512,256]{3,2,1,0:T(8,128)S(1)} %copy-done.3, f32[2,256,256]{2,1,0:T(8,128)S(1)} %collective-permute-done.10.lower, ...), custom_call_target="tpu_custom_call" | custom-call | flops 10000000000 | bytes 12582912 | tf_op jit(solution)/shard_map/turn/pallas_call | solution.py:288
  101.7 6.2 %backward.3 = (f32[2,512,256]{2,1,0:T(8,128)S(1)}, f32[2,256,256]{2,1,0:T(8,128)S(1)}, f32[2,768,256]{2,1,0:T(8,128)S(1)}, f32[3,2,256,256]{3,2,1,0:T(8,128)S(1)}) custom-call(s32[3,2]{1,0:T(4,128)S(1)} %copy.16.pos, f32[3,2,256,256]{3,2,1,0:T(8,128)S(1)} %get-tuple-element.81.slab, f32[3,2,256,256]{3,2,1,0:T(8,128)S(1)} %get-tuple-element.80.refs_2_.wave, ...), custom_call_target="tpu_custom_call" | custom-call | flops 10000000000 | bytes 12582912 | tf_op jit(solution)/shard_map/backward/pallas_call | solution.py:308
  109.1 6.2 %backward.4 = (f32[2,512,256]{2,1,0:T(8,128)S(1)}, f32[2,256,256]{2,1,0:T(8,128)S(1)}, f32[2,768,256]{2,1,0:T(8,128)S(1)}, f32[3,2,256,256]{3,2,1,0:T(8,128)S(1)}) custom-call(s32[3,2]{1,0:T(4,128)S(1)} %copy.16.pos, f32[3,2,256,256]{3,2,1,0:T(8,128)S(1)} %get-tuple-element.79.slab, f32[3,2,256,256]{3,2,1,0:T(8,128)S(1)} %get-tuple-element.78.refs_2_.wave, ...), custom_call_target="tpu_custom_call" | custom-call | flops 10000000000 | bytes 12582912 | tf_op jit(solution)/shard_map/backward/pallas_call | solution.py:308
  116.4 6.3 %backward.5 = (f32[2,512,256]{2,1,0:T(8,128)S(1)}, f32[2,256,256]{2,1,0:T(8,128)S(1)}, f32[2,512,256]{2,1,0:T(8,128)S(1)}, f32[2,256,256]{2,1,0:T(8,128)S(1)}, f32[1,2,256,256]{3,2,1,0:T(8,128)S(1)}) custom-call(s32[3,2]{1,0:T(4,128)S(1)} %copy.16.pos, f32[3,2,256,256]{3,2,1,0:T(8,128)S(1)} %get-tuple-element.76.slab, f32[1,2,256,256]{3,2,1,0:T(8,128)S(1)} %bitcast.72, ...), custom_call_target="tpu_custom_call" | custom-call | flops 10000000000 | bytes 12582912 | tf_op jit(solution)/shard_map/backward/pallas_call | solution.py:308
  129.9 5.3 %collective-permute-start.25 = (f32[64,256]{1,0:T(8,128)}, f32[64,256]{1,0:T(8,128)S(1)}, u32[]{:S(2)}, u32[]{:S(2)}) collective-permute-start(f32[64,256]{1,0:T(8,128)} %get-tuple-element.107), channel_id=1, source_target_pairs={{0,24},{1,25},{2,26},{3,27},{4,28},{5,29},{6,30},{7,31},{8,0},{9,1... | collective-permute-start | bytes 196616 | tf_op jit(solution)/shard_map/ppermute | solution.py:338
  135.9 2.7 %collective-permute-start.14 = (f32[2,256,256]{2,1,0:T(8,128)}, f32[2,256,256]{2,1,0:T(8,128)}, u32[]{:S(2)}, u32[]{:S(2)}) collective-permute-start(f32[2,256,256]{2,1,0:T(8,128)} %copy-done.20), channel_id=1, source_target_pairs={{0,1},{1,2},{2,3},{3,4},{4,5},{5,6},{6,7},{7,8},{8,9},{9,10},{10,1... | collective-permute-start | bytes 1572872 | tf_op jit(solution)/shard_map/ppermute | solution.py:22
  138.6 1.9 collective-permute-start.20
  141.8 3.1 %collective-permute-start.26 = (f32[64,256]{1,0:T(8,128)S(1)}, f32[64,256]{1,0:T(8,128)S(1)}, u32[]{:S(2)}, u32[]{:S(2)}) collective-permute-start(f32[64,256]{1,0:T(8,128)S(1)} %add_add_fusion), channel_id=1, source_target_pairs={{0,32},{1,33},{2,34},{3,35},{4,36},{5,37},{6,38},{7,39},{8,40},{9,... | collective-permute-start | bytes 196616 | tf_op jit(solution)/shard_map/ppermute | solution.py:338
  144.8 1.7 collective-permute-done.26
  146.5 3.3 %collective-permute-start.27 = (f32[64,256]{1,0:T(8,128)S(1)}, f32[64,256]{1,0:T(8,128)S(1)}, u32[]{:S(2)}, u32[]{:S(2)}) collective-permute-start(f32[64,256]{1,0:T(8,128)S(1)} %add.190), channel_id=1, source_target_pairs={{0,64},{1,65},{2,66},{3,67},{4,68},{5,69},{6,70},{7,71},{8,72},{9,... | collective-permute-start | bytes 196616 | tf_op jit(solution)/shard_map/ppermute | solution.py:338
  149.8 5.1 %collective-permute-start.13 = (f32[2,512,256]{2,1,0:T(8,128)}, f32[2,512,256]{2,1,0:T(8,128)}, u32[]{:S(2)}, u32[]{:S(2)}) collective-permute-start(f32[2,512,256]{2,1,0:T(8,128)} %copy-done.18), channel_id=1, source_target_pairs={{0,1},{1,2},{2,3},{3,4},{4,5},{5,6},{6,7},{7,8},{8,9},{9,10},{10,1... | collective-permute-start | bytes 3145736 | tf_op jit(solution)/shard_map/ppermute | solution.py:22
  154.9 3.7 %collective-permute-start.28 = (f32[64,256]{1,0:T(8,128)S(1)}, f32[64,256]{1,0:T(8,128)S(1)}, u32[]{:S(2)}, u32[]{:S(2)}) collective-permute-start(f32[64,256]{1,0:T(8,128)S(1)} %add.191), channel_id=1, source_target_pairs={{0,2},{1,3},{2,0},{3,1},{4,6},{5,7},{6,4},{7,5},{8,10},{9,11},{10,... | collective-permute-start | bytes 196616 | tf_op jit(solution)/shard_map/ppermute | solution.py:338
  158.7 16.4 %collective-permute-done.28 = f32[64,256]{1,0:T(8,128)S(1)} collective-permute-done((f32[64,256]{1,0:T(8,128)S(1)}, f32[64,256]{1,0:T(8,128)S(1)}, u32[]{:S(2)}, u32[]{:S(2)}) %collective-permute-start.28) | collective-permute-done | bytes 65568 | tf_op jit(solution)/shard_map/ppermute | solution.py:338
  175.1 5.4 %collective-permute-start.29 = (f32[64,256]{1,0:T(8,128)S(1)}, f32[64,256]{1,0:T(8,128)S(1)}, u32[]{:S(2)}, u32[]{:S(2)}) collective-permute-start(f32[64,256]{1,0:T(8,128)S(1)} %add.192), channel_id=1, source_target_pairs={{0,4},{1,5},{2,6},{3,7},{4,0},{5,1},{6,2},{7,3},{8,12},{9,13},{10,... | collective-permute-start | bytes 196616 | tf_op jit(solution)/shard_map/ppermute | solution.py:338
  180.5 2.0 collective-permute-start.18
  183.7 5.0 %collective-permute-start.15 = (f32[2,256,256]{2,1,0:T(8,128)S(1)}, f32[2,256,256]{2,1,0:T(8,128)S(1)}, u32[]{:S(2)}, u32[]{:S(2)}) collective-permute-start(f32[2,256,256]{2,1,0:T(8,128)S(1)} %add.165), channel_id=1, source_target_pairs={{0,32},{32,64},{64,96},{1,33},{33,65},{65,97},{2,34},{34,66},{66,9... | collective-permute-start | bytes 1572872 | tf_op jit(solution)/shard_map/ppermute | solution.py:22
  188.9 4.3 %collective-permute-done.30 = f32[64,256]{1,0:T(8,128)S(1)} collective-permute-done((f32[64,256]{1,0:T(8,128)S(1)}, f32[64,256]{1,0:T(8,128)S(1)}, u32[]{:S(2)}, u32[]{:S(2)}) %collective-permute-start.30) | collective-permute-done | bytes 65568 | tf_op jit(solution)/shard_map/ppermute | solution.py:338
  193.6 4.2 %collective-permute-done.31 = f32[64,256]{1,0:T(8,128)S(1)} collective-permute-done((f32[64,256]{1,0:T(8,128)S(1)}, f32[64,256]{1,0:T(8,128)S(1)}, u32[]{:S(2)}, u32[]{:S(2)}) %collective-permute-start.31) | collective-permute-done | bytes 65568 | tf_op jit(solution)/shard_map/ppermute | solution.py:338
  199.2 1.7 collective-permute-done.32
  200.9 4.4 %collective-permute-start.33 = (f32[256,256]{1,0:T(8,128)S(1)}, f32[256,256]{1,0:T(8,128)S(1)}, u32[]{:S(2)}, u32[]{:S(2)}) collective-permute-start(f32[256,256]{1,0:T(8,128)S(1)} %constant_dynamic-update-slice_fusion), channel_id=1, source_target_pairs={{0,1},{1,0},{2,3},{3,2},{4,5},{5,4},{6,7},{7,6},{8,9},{9,8},{10,11... | collective-permute-start | bytes 786440 | tf_op jit(solution)/shard_map/ppermute | solution.py:338
  206.5 3.4 %collective-permute-start.16 = (f32[2,768,256]{2,1,0:T(8,128)S(1)}, f32[2,768,256]{2,1,0:T(8,128)S(1)}, u32[]{:S(2)}, u32[]{:S(2)}) collective-permute-start(f32[2,768,256]{2,1,0:T(8,128)S(1)} %copy-done.15), channel_id=1, source_target_pairs={{0,1},{1,2},{2,3},{3,4},{4,5},{5,6},{6,7},{7,8},{8,9},{9,10},{10,1... | collective-permute-start | bytes 4718600 | tf_op jit(solution)/shard_map/ppermute | solution.py:22
  216.8 3.5 %collective-permute-start.21 = (f32[2,256,256]{2,1,0:T(8,128)S(1)}, f32[2,256,256]{2,1,0:T(8,128)S(1)}, u32[]{:S(2)}, u32[]{:S(2)}) collective-permute-start(f32[2,256,256]{2,1,0:T(8,128)S(1)} %slice_add_fusion.3), channel_id=1, source_target_pairs={{0,32},{32,64},{64,96},{1,33},{33,65},{65,97},{2,34},{34,66},{66,9... | collective-permute-start | bytes 1572872 | tf_op jit(solution)/shard_map/ppermute | solution.py:22
  221.6 3.1 %collective-permute-start.19 = (f32[2,256,256]{2,1,0:T(8,128)S(1)}, f32[2,256,256]{2,1,0:T(8,128)S(1)}, u32[]{:S(2)}, u32[]{:S(2)}) collective-permute-start(f32[2,256,256]{2,1,0:T(8,128)S(1)} %slice_add_fusion.5), channel_id=1, source_target_pairs={{0,32},{32,64},{64,96},{1,33},{33,65},{65,97},{2,34},{34,66},{66,9... | collective-permute-start | bytes 1572872 | tf_op jit(solution)/shard_map/ppermute | solution.py:22
  224.7 2.5 collective-permute-done.16
  227.5 3.5 %collective-permute-start.17 = (f32[2,256,256]{2,1,0:T(8,128)S(1)}, f32[2,256,256]{2,1,0:T(8,128)S(1)}, u32[]{:S(2)}, u32[]{:S(2)}) collective-permute-start(f32[2,256,256]{2,1,0:T(8,128)S(1)} %slice_add_fusion.7), channel_id=1, source_target_pairs={{0,32},{32,64},{64,96},{1,33},{33,65},{65,97},{2,34},{34,66},{66,9... | collective-permute-start | bytes 1572872 | tf_op jit(solution)/shard_map/ppermute | solution.py:22
  232.1 11.2 %collective-permute-done.19 = f32[2,256,256]{2,1,0:T(8,128)S(1)} collective-permute-done((f32[2,256,256]{2,1,0:T(8,128)S(1)}, f32[2,256,256]{2,1,0:T(8,128)S(1)}, u32[]{:S(2)}, u32[]{:S(2)}) %collective-permute-start.19) | collective-permute-done | bytes 524320 | tf_op jit(solution)/shard_map/ppermute | solution.py:22
  243.3 10.8 %collective-permute-done.17 = f32[2,256,256]{2,1,0:T(8,128)S(1)} collective-permute-done((f32[2,256,256]{2,1,0:T(8,128)S(1)}, f32[2,256,256]{2,1,0:T(8,128)S(1)}, u32[]{:S(2)}, u32[]{:S(2)}) %collective-permute-start.17) | collective-permute-done | bytes 524320 | tf_op jit(solution)/shard_map/ppermute | solution.py:22
  254.1 2.5 pad_maximum_fusion
  (129 shorter events, 39.8 us)
Async XLA Ops:
  0.6 27.1 %copy-start = (f32[3,256,256]{2,1,0:T(8,128)S(1)}, f32[3,256,256]{2,1,0:T(8,128)}, u32[]{:S(2)}) copy-start(f32[3,256,256]{2,1,0:T(8,128)} %param.20) | copy-start | bytes 2359300
  3.0 44.9 %collective-permute-start.1 = (f32[2,512,256]{2,1,0:T(8,128)}, f32[2,512,256]{2,1,0:T(8,128)}, u32[]{:S(2)}, u32[]{:S(2)}) collective-permute-start(f32[2,512,256]{2,1,0:T(8,128)} %slice_bitcast_fusion.3), channel_id=1, source_target_pairs={{1,0},{2,1},{3,2},{4,3},{5,4},{6,5},{7,6},{8,7},{9,8},{10,9},{11,1... | collective-permute-start | bytes 3145736 | tf_op jit(solution)/shard_map/ppermute | solution.py:22
  6.3 8.6 %copy-start.2 = (f32[4,2,512,256]{3,2,1,0:T(8,128)S(1)}, f32[4,2,512,256]{3,2,1,0:T(8,128)}, u32[]{:S(2)}) copy-start(f32[4,2,512,256]{3,2,1,0:T(8,128)} %own.7) | copy-start | bytes 12582916
  8.4 17.4 %collective-permute-start = (f32[2,256,256]{2,1,0:T(8,128)}, f32[2,256,256]{2,1,0:T(8,128)S(1)}, u32[]{:S(2)}, u32[]{:S(2)}) collective-permute-start(f32[2,256,256]{2,1,0:T(8,128)} %slice_bitcast_fusion.7), channel_id=1, source_target_pairs={{32,0},{64,32},{96,64},{33,1},{65,33},{97,65},{34,2},{66,34},{98,6... | collective-permute-start | bytes 1572872 | tf_op jit(solution)/shard_map/ppermute | solution.py:22
  12.2 46.5 %collective-permute-start.10 = (f32[2,256,256]{2,1,0:T(8,128)}, f32[2,256,256]{2,1,0:T(8,128)S(1)}, u32[]{:S(2)}, u32[]{:S(2)}) collective-permute-start(f32[2,256,256]{2,1,0:T(8,128)} %get-tuple-element.104), channel_id=1, source_target_pairs={{32,0},{64,32},{96,64},{33,1},{65,33},{97,65},{34,2},{66,34},{98,6... | collective-permute-start | bytes 1572872 | tf_op jit(solution)/shard_map/ppermute | solution.py:22
  13.5 5.2 %copy-start.26 = (f32[256,256]{1,0:T(8,128)S(1)}, f32[256,256]{1,0:T(8,128)}, u32[]{:S(2)}) copy-start(f32[256,256]{1,0:T(8,128)} %param.17) | copy-start | bytes 786436
  13.5 6.0 %copy-start.25 = (s32[3,2]{0,1:T(2,128)S(1)}, s32[3,2]{0,1:T(2,128)}, u32[]{:S(2)}) copy-start(s32[3,2]{0,1:T(2,128)} %param.18) | copy-start | bytes 76
  13.5 33.1 %collective-permute-start.3 = (f32[2,256,256]{2,1,0:T(8,128)}, f32[2,256,256]{2,1,0:T(8,128)}, u32[]{:S(2)}, u32[]{:S(2)}) collective-permute-start(f32[2,256,256]{2,1,0:T(8,128)} %get-tuple-element.103), channel_id=1, source_target_pairs={{32,0},{64,32},{96,64},{33,1},{65,33},{97,65},{34,2},{66,34},{98,6... | collective-permute-start | bytes 1572872 | tf_op jit(solution)/shard_map/ppermute | solution.py:22
  16.7 16.6 %collective-permute-start.4 = (f32[2,512,256]{2,1,0:T(8,128)}, f32[2,512,256]{2,1,0:T(8,128)S(1)}, u32[]{:S(2)}, u32[]{:S(2)}) collective-permute-start(f32[2,512,256]{2,1,0:T(8,128)} %get-tuple-element.100), channel_id=1, source_target_pairs={{1,0},{2,1},{3,2},{4,3},{5,4},{6,5},{7,6},{8,7},{9,8},{10,9},{11,1... | collective-permute-start | bytes 3145736 | tf_op jit(solution)/shard_map/ppermute | solution.py:22
  24.4 8.9 %copy-start.22 = (f32[2,512,256]{2,1,0:T(8,128)S(1)}, f32[2,512,256]{2,1,0:T(8,128)}, u32[]{:S(2)}) copy-start(f32[2,512,256]{2,1,0:T(8,128)} %get-tuple-element.101) | copy-start | bytes 3145732
  24.4 22.2 %copy-start.24 = (f32[2,256,256]{2,1,0:T(8,128)S(1)}, f32[2,256,256]{2,1,0:T(8,128)}, u32[]{:S(2)}) copy-start(f32[2,256,256]{2,1,0:T(8,128)} %get-tuple-element.105) | copy-start | bytes 1572868
  24.4 27.2 %copy-start.19 = (f32[2,256,256]{2,1,0:T(8,128)S(1)}, f32[2,256,256]{2,1,0:T(8,128)}, u32[]{:S(2)}) copy-start(f32[2,256,256]{2,1,0:T(8,128)} %param.16) | copy-start | bytes 1572868
  25.8 24.5 %collective-permute-start.2 = (f32[2,256,256]{2,1,0:T(8,128)S(1)}, f32[2,256,256]{2,1,0:T(8,128)S(1)}, u32[]{:S(2)}, u32[]{:S(2)}) collective-permute-start(f32[2,256,256]{2,1,0:T(8,128)S(1)} %collective-permute-done.lower), channel_id=1, source_target_pairs={{1,0},{2,1},{3,2},{4,3},{5,4},{6,5},{7,6},{8,7},{9,8},{10,9},{11,1... | collective-permute-start | bytes 1572872 | tf_op jit(solution)/shard_map/ppermute | solution.py:22
  27.7 23.9 %copy-start.3 = (f32[4,2,512,256]{3,2,1,0:T(8,128)S(1)}, f32[4,2,512,256]{3,2,1,0:T(8,128)}, u32[]{:S(2)}) copy-start(f32[4,2,512,256]{3,2,1,0:T(8,128)} %own.7) | copy-start | bytes 12582916
  33.3 58.5 %collective-permute-start.11 = (f32[2,512,256]{2,1,0:T(8,128)S(1)}, f32[2,512,256]{2,1,0:T(8,128)S(1)}, u32[]{:S(2)}, u32[]{:S(2)}) collective-permute-start(f32[2,512,256]{2,1,0:T(8,128)S(1)} %copy-done.22), channel_id=1, source_target_pairs={{1,0},{2,1},{3,2},{4,3},{5,4},{6,5},{7,6},{8,7},{9,8},{10,9},{11,1... | collective-permute-start | bytes 3145736 | tf_op jit(solution)/shard_map/ppermute | solution.py:22
  46.7 15.0 %collective-permute-start.7 = (f32[2,256,256]{2,1,0:T(8,128)S(1)}, f32[2,256,256]{2,1,0:T(8,128)S(1)}, u32[]{:S(2)}, u32[]{:S(2)}) collective-permute-start(f32[2,256,256]{2,1,0:T(8,128)S(1)} %copy-done.24), channel_id=1, source_target_pairs={{32,0},{64,32},{96,64},{33,1},{65,33},{97,65},{34,2},{66,34},{98,6... | collective-permute-start | bytes 1572872 | tf_op jit(solution)/shard_map/ppermute | solution.py:22
  48.0 17.7 %collective-permute-start.6 = (f32[2,256,256]{2,1,0:T(8,128)}, f32[2,256,256]{2,1,0:T(8,128)S(1)}, u32[]{:S(2)}, u32[]{:S(2)}) collective-permute-start(f32[2,256,256]{2,1,0:T(8,128)} %collective-permute-done.3.lower), channel_id=1, source_target_pairs={{1,0},{3,2},{5,4},{7,6},{9,8},{11,10},{13,12},{15,14},{17,16},{19,... | collective-permute-start | bytes 1572872 | tf_op jit(solution)/shard_map/ppermute | solution.py:382
  50.3 17.5 %collective-permute-start.5 = (f32[2,256,256]{2,1,0:T(8,128)S(1)}, f32[2,256,256]{2,1,0:T(8,128)S(1)}, u32[]{:S(2)}, u32[]{:S(2)}) collective-permute-start(f32[2,256,256]{2,1,0:T(8,128)S(1)} %slice.172), channel_id=1, source_target_pairs={{33,1},{35,3},{37,5},{39,7},{41,9},{43,11},{45,13},{47,15},{49,17}... | collective-permute-start | bytes 1572872 | tf_op jit(solution)/shard_map/ppermute | solution.py:381
  51.6 7.1 %copy-start.23 = (f32[2,512,256]{2,1,0:T(8,128)S(1)}, f32[2,512,256]{2,1,0:T(8,128)}, u32[]{:S(2)}) copy-start(f32[2,512,256]{2,1,0:T(8,128)} %get-tuple-element.102) | copy-start | bytes 3145732
  58.7 16.1 %collective-permute-start.8 = (f32[2,512,256]{2,1,0:T(8,128)S(1)}, f32[2,512,256]{2,1,0:T(8,128)S(1)}, u32[]{:S(2)}, u32[]{:S(2)}) collective-permute-start(f32[2,512,256]{2,1,0:T(8,128)S(1)} %copy-done.23), channel_id=1, source_target_pairs={{1,0},{2,1},{3,2},{4,3},{5,4},{6,5},{7,6},{8,7},{9,8},{10,9},{11,1... | collective-permute-start | bytes 3145736 | tf_op jit(solution)/shard_map/ppermute | solution.py:22
  61.6 30.2 %collective-permute-start.12 = (f32[2,256,256]{2,1,0:T(8,128)S(1)}, f32[2,256,256]{2,1,0:T(8,128)S(1)}, u32[]{:S(2)}, u32[]{:S(2)}) collective-permute-start(f32[2,256,256]{2,1,0:T(8,128)S(1)} %collective-permute-done.10.lower), channel_id=1, source_target_pairs={{1,0},{2,1},{3,2},{4,3},{5,4},{6,5},{7,6},{8,7},{9,8},{10,9},{11,1... | collective-permute-start | bytes 1572872 | tf_op jit(solution)/shard_map/ppermute | solution.py:22
  65.6 20.4 %collective-permute-start.9 = (f32[2,256,256]{2,1,0:T(8,128)S(1)}, f32[2,256,256]{2,1,0:T(8,128)S(1)}, u32[]{:S(2)}, u32[]{:S(2)}) collective-permute-start(f32[2,256,256]{2,1,0:T(8,128)S(1)} %collective-permute-done.7.lower), channel_id=1, source_target_pairs={{1,0},{2,1},{3,2},{4,3},{5,4},{6,5},{7,6},{8,7},{9,8},{10,9},{11,1... | collective-permute-start | bytes 1572872 | tf_op jit(solution)/shard_map/ppermute | solution.py:22
  109.1 6.2 %copy-start.8 = (f32[2,256,256]{2,1,0:T(8,128)}, f32[2,256,256]{2,1,0:T(8,128)S(1)}, u32[]{:S(2)}) copy-start(f32[2,256,256]{2,1,0:T(8,128)S(1)} %get-tuple-element.95) | copy-start | bytes 1572868
  126.5 1.7 collective-permute-start.22
  129.2 53.3 %copy-start.13 = (f32[2,256,256]{2,1,0:T(8,128)S(1)}, f32[2,256,256]{2,1,0:T(8,128)}, u32[]{:S(2)}) copy-start(f32[2,256,256]{2,1,0:T(8,128)} %copy-done.12) | copy-start | bytes 1572868
  129.9 10.6 %collective-permute-start.25 = (f32[64,256]{1,0:T(8,128)}, f32[64,256]{1,0:T(8,128)S(1)}, u32[]{:S(2)}, u32[]{:S(2)}) collective-permute-start(f32[64,256]{1,0:T(8,128)} %get-tuple-element.107), channel_id=1, source_target_pairs={{0,24},{1,25},{2,26},{3,27},{4,28},{5,29},{6,30},{7,31},{8,0},{9,1... | collective-permute-start | bytes 196616 | tf_op jit(solution)/shard_map/ppermute | solution.py:338
  135.2 5.3 %collective-permute-start.24 = (f32[64,256]{1,0:T(8,128)}, f32[64,256]{1,0:T(8,128)S(1)}, u32[]{:S(2)}, u32[]{:S(2)}) collective-permute-start(f32[64,256]{1,0:T(8,128)} %get-tuple-element.108), channel_id=1, source_target_pairs={{0,16},{1,17},{2,18},{3,19},{4,20},{5,21},{6,22},{7,23},{8,24},{9,... | collective-permute-start | bytes 196616 | tf_op jit(solution)/shard_map/ppermute | solution.py:338
  135.2 5.7 %collective-permute-start.23 = (f32[64,256]{1,0:T(8,128)}, f32[64,256]{1,0:T(8,128)}, u32[]{:S(2)}, u32[]{:S(2)}) collective-permute-start(f32[64,256]{1,0:T(8,128)} %get-tuple-element.106), channel_id=1, source_target_pairs={{0,8},{1,9},{2,10},{3,11},{4,12},{5,13},{6,14},{7,15},{8,16},{9,17... | collective-permute-start | bytes 196616 | tf_op jit(solution)/shard_map/ppermute | solution.py:338
  135.9 46.6 %collective-permute-start.14 = (f32[2,256,256]{2,1,0:T(8,128)}, f32[2,256,256]{2,1,0:T(8,128)}, u32[]{:S(2)}, u32[]{:S(2)}) collective-permute-start(f32[2,256,256]{2,1,0:T(8,128)} %copy-done.20), channel_id=1, source_target_pairs={{0,1},{1,2},{2,3},{3,4},{4,5},{5,6},{6,7},{7,8},{8,9},{9,10},{10,1... | collective-permute-start | bytes 1572872 | tf_op jit(solution)/shard_map/ppermute | solution.py:22
  138.6 73.7 %collective-permute-start.20 = (f32[2,768,256]{2,1,0:T(8,128)}, f32[2,768,256]{2,1,0:T(8,128)}, u32[]{:S(2)}, u32[]{:S(2)}) collective-permute-start(f32[2,768,256]{2,1,0:T(8,128)} %copy-done.17), channel_id=1, source_target_pairs={{0,1},{1,2},{2,3},{3,4},{4,5},{5,6},{6,7},{7,8},{8,9},{9,10},{10,1... | collective-permute-start | bytes 4718600 | tf_op jit(solution)/shard_map/ppermute | solution.py:22
  141.8 4.7 %collective-permute-start.26 = (f32[64,256]{1,0:T(8,128)S(1)}, f32[64,256]{1,0:T(8,128)S(1)}, u32[]{:S(2)}, u32[]{:S(2)}) collective-permute-start(f32[64,256]{1,0:T(8,128)S(1)} %add_add_fusion), channel_id=1, source_target_pairs={{0,32},{1,33},{2,34},{3,35},{4,36},{5,37},{6,38},{7,39},{8,40},{9,... | collective-permute-start | bytes 196616 | tf_op jit(solution)/shard_map/ppermute | solution.py:338
  146.5 8.4 %collective-permute-start.27 = (f32[64,256]{1,0:T(8,128)S(1)}, f32[64,256]{1,0:T(8,128)S(1)}, u32[]{:S(2)}, u32[]{:S(2)}) collective-permute-start(f32[64,256]{1,0:T(8,128)S(1)} %add.190), channel_id=1, source_target_pairs={{0,64},{1,65},{2,66},{3,67},{4,68},{5,69},{6,70},{7,71},{8,72},{9,... | collective-permute-start | bytes 196616 | tf_op jit(solution)/shard_map/ppermute | solution.py:338
  149.8 60.9 %collective-permute-start.13 = (f32[2,512,256]{2,1,0:T(8,128)}, f32[2,512,256]{2,1,0:T(8,128)}, u32[]{:S(2)}, u32[]{:S(2)}) collective-permute-start(f32[2,512,256]{2,1,0:T(8,128)} %copy-done.18), channel_id=1, source_target_pairs={{0,1},{1,2},{2,3},{3,4},{4,5},{5,6},{6,7},{7,8},{8,9},{9,10},{10,1... | collective-permute-start | bytes 3145736 | tf_op jit(solution)/shard_map/ppermute | solution.py:22
  154.9 20.2 %collective-permute-start.28 = (f32[64,256]{1,0:T(8,128)S(1)}, f32[64,256]{1,0:T(8,128)S(1)}, u32[]{:S(2)}, u32[]{:S(2)}) collective-permute-start(f32[64,256]{1,0:T(8,128)S(1)} %add.191), channel_id=1, source_target_pairs={{0,2},{1,3},{2,0},{3,1},{4,6},{5,7},{6,4},{7,5},{8,10},{9,11},{10,... | collective-permute-start | bytes 196616 | tf_op jit(solution)/shard_map/ppermute | solution.py:338
  175.1 13.7 %collective-permute-start.29 = (f32[64,256]{1,0:T(8,128)S(1)}, f32[64,256]{1,0:T(8,128)S(1)}, u32[]{:S(2)}, u32[]{:S(2)}) collective-permute-start(f32[64,256]{1,0:T(8,128)S(1)} %add.192), channel_id=1, source_target_pairs={{0,4},{1,5},{2,6},{3,7},{4,0},{5,1},{6,2},{7,3},{8,12},{9,13},{10,... | collective-permute-start | bytes 196616 | tf_op jit(solution)/shard_map/ppermute | solution.py:338
  180.5 26.0 %copy-start.15 = (f32[2,768,256]{2,1,0:T(8,128)S(1)}, f32[2,768,256]{2,1,0:T(8,128)}, u32[]{:S(2)}) copy-start(f32[2,768,256]{2,1,0:T(8,128)} %copy-done.14) | copy-start | bytes 4718596
  180.5 39.8 %collective-permute-start.18 = (f32[2,768,256]{2,1,0:T(8,128)}, f32[2,768,256]{2,1,0:T(8,128)S(1)}, u32[]{:S(2)}, u32[]{:S(2)}) collective-permute-start(f32[2,768,256]{2,1,0:T(8,128)} %copy-done.16), channel_id=1, source_target_pairs={{0,1},{1,2},{2,3},{3,4},{4,5},{5,6},{6,7},{7,8},{8,9},{9,10},{10,1... | collective-permute-start | bytes 4718600 | tf_op jit(solution)/shard_map/ppermute | solution.py:22
  182.5 28.2 %copy-start.7 = (f32[2,512,256]{2,1,0:T(8,128)S(1)}, f32[2,512,256]{2,1,0:T(8,128)}, u32[]{:S(2)}) copy-start(f32[2,512,256]{2,1,0:T(8,128)} %copy-done.6) | copy-start | bytes 3145732
  183.7 28.4 %collective-permute-start.15 = (f32[2,256,256]{2,1,0:T(8,128)S(1)}, f32[2,256,256]{2,1,0:T(8,128)S(1)}, u32[]{:S(2)}, u32[]{:S(2)}) collective-permute-start(f32[2,256,256]{2,1,0:T(8,128)S(1)} %add.165), channel_id=1, source_target_pairs={{0,32},{32,64},{64,96},{1,33},{33,65},{65,97},{2,34},{34,66},{66,9... | collective-permute-start | bytes 1572872 | tf_op jit(solution)/shard_map/ppermute | solution.py:22
  188.8 4.4 %collective-permute-start.30 = (f32[64,256]{1,0:T(8,128)S(1)}, f32[64,256]{1,0:T(8,128)S(1)}, u32[]{:S(2)}, u32[]{:S(2)}) collective-permute-start(f32[64,256]{1,0:T(8,128)S(1)} %add.193), channel_id=1, source_target_pairs={{0,8},{1,9},{2,10},{3,11},{4,12},{5,13},{6,14},{7,15},{8,16},{9,17... | collective-permute-start | bytes 196616 | tf_op jit(solution)/shard_map/ppermute | solution.py:338
  193.2 4.6 %collective-permute-start.31 = (f32[64,256]{1,0:T(8,128)S(1)}, f32[64,256]{1,0:T(8,128)S(1)}, u32[]{:S(2)}, u32[]{:S(2)}) collective-permute-start(f32[64,256]{1,0:T(8,128)S(1)} %add.193), channel_id=1, source_target_pairs={{0,16},{1,17},{2,18},{3,19},{4,20},{5,21},{6,22},{7,23},{8,24},{9,... | collective-permute-start | bytes 196616 | tf_op jit(solution)/shard_map/ppermute | solution.py:338
  197.8 3.1 %collective-permute-start.32 = (f32[64,256]{1,0:T(8,128)S(1)}, f32[64,256]{1,0:T(8,128)S(1)}, u32[]{:S(2)}, u32[]{:S(2)}) collective-permute-start(f32[64,256]{1,0:T(8,128)S(1)} %add.193), channel_id=1, source_target_pairs={{0,24},{1,25},{2,26},{3,27},{4,28},{5,29},{6,30},{7,31},{8,0},{9,1... | collective-permute-start | bytes 196616 | tf_op jit(solution)/shard_map/ppermute | solution.py:338
  200.9 5.6 %collective-permute-start.33 = (f32[256,256]{1,0:T(8,128)S(1)}, f32[256,256]{1,0:T(8,128)S(1)}, u32[]{:S(2)}, u32[]{:S(2)}) collective-permute-start(f32[256,256]{1,0:T(8,128)S(1)} %constant_dynamic-update-slice_fusion), channel_id=1, source_target_pairs={{0,1},{1,0},{2,3},{3,2},{4,5},{5,4},{6,7},{7,6},{8,9},{9,8},{10,11... | collective-permute-start | bytes 786440 | tf_op jit(solution)/shard_map/ppermute | solution.py:338
  206.5 20.7 %collective-permute-start.16 = (f32[2,768,256]{2,1,0:T(8,128)S(1)}, f32[2,768,256]{2,1,0:T(8,128)S(1)}, u32[]{:S(2)}, u32[]{:S(2)}) collective-permute-start(f32[2,768,256]{2,1,0:T(8,128)S(1)} %copy-done.15), channel_id=1, source_target_pairs={{0,1},{1,2},{2,3},{3,4},{4,5},{5,6},{6,7},{7,8},{8,9},{9,10},{10,1... | collective-permute-start | bytes 4718600 | tf_op jit(solution)/shard_map/ppermute | solution.py:22
  216.8 15.2 %collective-permute-start.21 = (f32[2,256,256]{2,1,0:T(8,128)S(1)}, f32[2,256,256]{2,1,0:T(8,128)S(1)}, u32[]{:S(2)}, u32[]{:S(2)}) collective-permute-start(f32[2,256,256]{2,1,0:T(8,128)S(1)} %slice_add_fusion.3), channel_id=1, source_target_pairs={{0,32},{32,64},{64,96},{1,33},{33,65},{65,97},{2,34},{34,66},{66,9... | collective-permute-start | bytes 1572872 | tf_op jit(solution)/shard_map/ppermute | solution.py:22
  221.6 21.7 %collective-permute-start.19 = (f32[2,256,256]{2,1,0:T(8,128)S(1)}, f32[2,256,256]{2,1,0:T(8,128)S(1)}, u32[]{:S(2)}, u32[]{:S(2)}) collective-permute-start(f32[2,256,256]{2,1,0:T(8,128)S(1)} %slice_add_fusion.5), channel_id=1, source_target_pairs={{0,32},{32,64},{64,96},{1,33},{33,65},{65,97},{2,34},{34,66},{66,9... | collective-permute-start | bytes 1572872 | tf_op jit(solution)/shard_map/ppermute | solution.py:22
  227.5 26.6 %collective-permute-start.17 = (f32[2,256,256]{2,1,0:T(8,128)S(1)}, f32[2,256,256]{2,1,0:T(8,128)S(1)}, u32[]{:S(2)}, u32[]{:S(2)}) collective-permute-start(f32[2,256,256]{2,1,0:T(8,128)S(1)} %slice_add_fusion.7), channel_id=1, source_target_pairs={{0,32},{32,64},{64,96},{1,33},{33,65},{65,97},{2,34},{34,66},{66,9... | collective-permute-start | bytes 1572872 | tf_op jit(solution)/shard_map/ppermute | solution.py:22
  254.1 2.5 copy-start.1
  (13 other events, 14.4 us)
